TPU v7x, 32 devices: a whole 2x2x4 slice. The times are simulated.
32 devices in a mesh: groups: 1, dp: 16 (over z, y, x), tp: 2 (over core).
Axes of the slice: x: 2, y: 2, z: 4, core: 2. Of those that a mesh axis runs over, the one named last changes fastest.
Arguments:
- pool: bfloat16 [2048, 4608], P(('groups', 'dp')), may hold values from -10 to 10
- page_holder: int32 [896], P(('groups', 'dp')), may hold values from 0 to 15, as said below
- page_slot: int32 [896], P(('groups', 'dp')), may hold values from 0 to 127
- suffix_latent_rows: bfloat16 [16, 9216], P(('groups', 'dp')), may hold values from -5 to 5
- prefill_queries: bfloat16 [16, 128, 4608], P(('groups', 'dp'), None, 'tp'), may hold values from -10 to 10
- suffix_len: int32 [2], P('groups'), may hold values from 1 to 128
- decode_queries: bfloat16 [64, 36864], P(('groups', 'dp'), 'tp'), may hold values from -10 to 10
- decode_len: int32 [64], P(('groups', 'dp')), may hold values from 1 to 256
Outputs:
- prefill_output: bfloat16 [16, 128, 4096], P(('groups', 'dp'), None, 'tp')
- decode_out: bfloat16 [64, 32768], P(('groups', 'dp'), 'tp')
Inputs may be any that keep to these rules, and one draw needn't show every extreme that they name: `page_holder`: within one device's 56 entries no holder appears more than 4 times, and some holder appears exactly 4 times.
All inputs are finite; a program needn't handle non-finite values.
Results may differ from a plain program's by a relative error of at most 0.004.
Values may be sent and summed in bfloat16 or wider, within the bound.
No kernel may reach another device: no remote copies, remote signals or barrier semaphores. Data moves between devices by JAX's collectives and lax.ppermute only.
A program may use at most 64 MiB of HBM per device.

v0:
```python
import math

import jax
import jax.numpy as jnp
from jax import lax
from jax.experimental import pallas as pl
from jax.experimental.pallas import tpu as pltpu
from jax.sharding import PartitionSpec as P


LATENT_WIDTH = 512
ROTARY_WIDTH = 64
WIDTH = LATENT_WIDTH + ROTARY_WIDTH
PADDED = 640
PAIR = 2 * WIDTH
TEAM = 8
LANES = 128
SUFFIX_LANES = 384
CHUNK = 128

softmax_scale = 192.0 ** (-0.5)
exp2_scale = softmax_scale * math.log2(math.e)
masked_score = -1e30


f32 = jnp.float32
bf16 = jnp.bfloat16


def iota(shape, dim):
    return lax.broadcasted_iota(jnp.int32, shape, dim)


def vmem():
    return pl.BlockSpec(memory_space=pltpu.VMEM)


def smem():
    return pl.BlockSpec(memory_space=pltpu.SMEM)


def call(body, n_smem, n_in, outs, mib=12, **kw):
    return pl.pallas_call(
        body,
        in_specs=[smem()] * n_smem + [vmem()] * n_in,
        out_specs=tuple(vmem() for _ in outs) if len(outs) > 1 else vmem(),
        out_shape=tuple(outs) if len(outs) > 1 else outs[0],
        compiler_params=pltpu.CompilerParams(vmem_limit_bytes=mib << 20),
        **kw,
    )


def xperm(value, masks):
    n, cores = lax.axis_size("dp"), lax.axis_size("tp")
    pairs = [(d * cores + c, (d ^ masks[c % 2]) * cores + c) for d in range(n) for c in range(cores)]
    return lax.ppermute(value, ("dp", "tp"), pairs)


def sibling(value):
    return lax.ppermute(value, "tp", [(0, 1), (1, 0)])


def request_table(holder, slot, ranks, cap, width):
    count = holder.shape[1]

    def body(h_hbm, s_hbm, out_ref, h_ref, s_ref, sems):
        copies = [
            pltpu.make_async_copy(h_hbm, h_ref, sems.at[0]),
            pltpu.make_async_copy(s_hbm, s_ref, sems.at[1]),
        ]
        for copy in copies:
            copy.start()
        for copy in copies:
            copy.wait()
        hrow = jnp.broadcast_to(h_ref[...], (count, count))
        srow = jnp.broadcast_to(s_ref[...], (count, count))
        i, j = iota((count, count), 0), iota((count, count), 1)
        hcol = jnp.sum(jnp.where(i == j, hrow, 0), axis=1, keepdims=True)
        scol = jnp.sum(jnp.where(i == j, srow, 0), axis=1, keepdims=True)
        rank = jnp.sum(jnp.where((hrow == hcol) & (j < i), 1, 0), axis=1, keepdims=True)
        lane = hcol * cap + rank
        hit = jnp.where(iota((count, width), 1) == lane, scol + 1, 0)
        row = jnp.sum(hit, axis=0, keepdims=True)
        out_ref[...] = jnp.where(iota((ranks, width), 0) == lax.axis_index("dp"), row, 0)

    return pl.pallas_call(
        body,
        in_specs=[pl.BlockSpec(memory_space=pltpu.HBM)] * 2,
        out_specs=vmem(),
        out_shape=jax.ShapeDtypeStruct((ranks, width), jnp.int32),
        scratch_shapes=[
            pltpu.VMEM((1, count), jnp.int32),
            pltpu.VMEM((1, count), jnp.int32),
            pltpu.SemaphoreType.DMA((2,)),
        ],
        compiler_params=pltpu.CompilerParams(vmem_limit_bytes=4 << 20),
    )(holder, slot)


def paired(page, page_width):
    out = []
    for b in range(0, page_width, PAIR):
        out.append(page[:, b : b + 512])
        out.append(page[:, b + 576 : b + 1088])
        out.append(jnp.concatenate([page[:, b + 512 : b + 576], page[:, b + 1088 : b + 1152]], axis=1))
    return jnp.concatenate(out, axis=1)


def prepare(queries, heads):
    tokens = queries.shape[0]

    def body(q_ref, qe_out, qo_out):
        zero = jnp.zeros((tokens, ROTARY_WIDTH), bf16)
        for h in range(heads):
            b = h * WIDTH
            nope = q_ref[:, b : b + 512]
            rope = q_ref[:, b + 512 : b + 576]
            rows = slice(h * tokens, (h + 1) * tokens)
            qe_out[rows, 0:512] = nope
            qo_out[rows, 0:512] = nope
            qe_out[rows, 512:640] = jnp.concatenate([rope, zero], axis=1)
            qo_out[rows, 512:640] = jnp.concatenate([zero, rope], axis=1)

    q_shape = jax.ShapeDtypeStruct((heads * tokens, PADDED), bf16)
    return call(body, 0, 1, [q_shape, q_shape])(queries)


def pair_pool(pool):
    def body(pool_ref, out_ref):
        out_ref[...] = paired(pool_ref[...], pool_ref.shape[1])

    return call(body, 0, 1, [jax.ShapeDtypeStruct(pool.shape, bf16)])(pool)


def stack_keys(page_ref, rows, page_width):
    pairs = page_width // PAIR
    even = jnp.concatenate([page_ref[rows, j * PAIR : j * PAIR + 512] for j in range(pairs)], axis=0)
    odd = jnp.concatenate([page_ref[rows, j * PAIR + 512 : j * PAIR + 1024] for j in range(pairs)], axis=0)
    rope = jnp.concatenate([page_ref[rows, j * PAIR + 1024 : j * PAIR + 1152] for j in range(pairs)], axis=0)
    return even, odd, rope


def dot_nt(a, b):
    return lax.dot_general(a, b, (((1,), (1,)), ((), ())), preferred_element_type=f32)


def decode(lens, pool, qe):
    rows, heads, _ = qe.shape
    pages, page_width = pool.shape
    per_row = pages // rows
    pairs = page_width // PAIR

    def body(len_ref, pool_ref, q_ref, out_ref):
        key_rows = pairs * per_row
        s = iota((heads, key_rows), 1)
        pos = (s % per_row) * (2 * pairs) + 2 * (s // per_row)
        zero = jnp.zeros((heads, ROTARY_WIDTH), bf16)
        done = []
        for g in range(rows):
            even, odd, rope = stack_keys(pool_ref, slice(g * per_row, (g + 1) * per_row), page_width)
            nope_q = q_ref[g, :, 0:512]
            rope_q = q_ref[g, :, 512:576]
            re = jnp.concatenate([rope_q, zero], axis=1)
            ro = jnp.concatenate([zero, rope_q], axis=1)
            se = dot_nt(nope_q, even) + dot_nt(re, rope)
            so = dot_nt(nope_q, odd) + dot_nt(ro, rope)
            se = jnp.where(pos < len_ref[g], se, masked_score)
            so = jnp.where(pos + 1 < len_ref[g], so, masked_score)
            peak = jnp.maximum(jnp.max(se, axis=1, keepdims=True), jnp.max(so, axis=1, keepdims=True))
            pe = jnp.exp2((se - peak) * exp2_scale)
            po = jnp.exp2((so - peak) * exp2_scale)
            den = jnp.sum(pe, axis=1, keepdims=True) + jnp.sum(po, axis=1, keepdims=True)
            out = jnp.dot(pe.astype(bf16), even, preferred_element_type=f32)
            out += jnp.dot(po.astype(bf16), odd, preferred_element_type=f32)
            done.append((out / den).astype(bf16))
        i, j = iota((rows * heads, rows * heads), 0), iota((rows * heads, rows * heads), 1)
        swap = jnp.where(j == (i % rows) * heads + i // rows, 1.0, 0.0).astype(bf16)
        done = jnp.dot(swap, jnp.concatenate(done, axis=0), preferred_element_type=f32)
        for h in range(heads):
            out_ref[:, h * LATENT_WIDTH : (h + 1) * LATENT_WIDTH] = done[h * rows : (h + 1) * rows, :].astype(bf16)

    return call(body, 1, 2, [jax.ShapeDtypeStruct((rows, heads * LATENT_WIDTH), bf16)])(lens, pool, qe)


def gather_pages(table, pool, suffix, streams, cap):
    ranks, width = table.shape
    pages, page_width = pool.shape
    block = TEAM * cap
    total = sum(half for _, half in streams)

    def body(table_ref, pool_ref, suffix_ref, *outs):
        me, core = lax.axis_index("dp"), lax.axis_index("tp")
        team = me // TEAM
        tab = table_ref[...].astype(f32).astype(bf16)

        def position(shape):
            n = iota(shape, 0)
            g = jnp.zeros(shape, jnp.int32)
            base = jnp.zeros(shape, jnp.int32)
            at = 0
            for first, half in streams:
                inside = (n >= at) & (n < at + half)
                g = jnp.where(inside, n - at + core * half, g)
                base = jnp.where(inside, first, base)
                at += half
            return base, g

        base, g = position((total, ranks))
        source = (team ^ (base + g // block)) * TEAM + (g % block) // cap
        pick = jnp.where(iota((total, ranks), 1) == source, 1.0, 0.0).astype(bf16)
        spread = jnp.dot(pick, tab, preferred_element_type=f32)
        _, g = position((total, width))
        mine = iota((total, width), 1) == me * cap + g % cap
        slot = jnp.sum(jnp.where(mine, spread, 0.0), axis=1, keepdims=True)
        hot = jnp.where(iota((total, pages), 1) + 1 == slot.astype(jnp.int32), 1.0, 0.0).astype(bf16)
        rows = jnp.dot(hot, pool_ref[...], preferred_element_type=f32).astype(bf16)
        at = 0
        for n, (_, half) in enumerate(streams):
            outs[n][:, 0:page_width] = rows[at : at + half]
            at += half
            if n == 0:
                left = suffix_ref[:, 0:SUFFIX_LANES]
                right = suffix_ref[:, SUFFIX_LANES : 2 * SUFFIX_LANES]
                if half > left.shape[0]:
                    outs[n][:, page_width:] = jnp.zeros((half, SUFFIX_LANES), bf16)
                outs[n][0 : left.shape[0], page_width:] = jnp.where(core == 0, left, right)

    outs = [
        jax.ShapeDtypeStruct((half, page_width + (SUFFIX_LANES if n == 0 else 0)), bf16)
        for n, (_, half) in enumerate(streams)
    ]
    out = call(body, 0, 3, outs)(table, pool, suffix)
    return out if len(outs) > 1 else (out,)


def key_masks(table, streams, cap, orders, tokens):
    ranks, width = table.shape
    block = TEAM * cap

    def body(table_ref, *outs):
        me, core = lax.axis_index("dp"), lax.axis_index("tp")
        team, member = me // TEAM, me % TEAM
        tab = table_ref[...].astype(f32).astype(bf16)
        for n, (base, half) in enumerate(streams):
            total = TEAM * half
            for side in range(2):
                owner = (core + side) % 2
                p = iota((width, total), 1)
                b, i = p // half, p % half
                away = jnp.zeros((width, total), jnp.int32)
                for k in range(3):
                    step = jnp.where(owner == 0, orders[n][0][k], orders[n][1][k])
                    away += ((b // (1 << k)) % 2) * step
                g = owner * half + i
                holder = (team ^ (base + g // block)) * TEAM + (member ^ away)
                sel = jnp.where(iota((width, total), 0) == holder * cap + g % cap, 1.0, 0.0).astype(bf16)
                q = iota((ranks, total), 1)
                asker = team * TEAM + ((owner * half + q % half) % block) // cap
                found = jnp.dot(tab, sel, preferred_element_type=f32)
                found = jnp.sum(jnp.where(iota((ranks, total), 0) == asker, found, 0.0), axis=0, keepdims=True)
                found = jnp.where(found > 0.0, 0.0, masked_score)
                for k in range(4):
                    wide = []
                    for at in range(k * 2 * half, (k + 1) * 2 * half, min(2 * half, CHUNK // 2)):
                        wide += [found[:, at : at + min(2 * half, CHUNK // 2)]] * tokens
                    outs[n][side * 4 + k : side * 4 + k + 1, :] = jnp.concatenate(wide, axis=1)

    outs = [jax.ShapeDtypeStruct((8, 2 * half * tokens), f32) for _, half in streams]
    out = call(body, 0, 1, outs)(table)
    return out if len(outs) > 1 else (out,)


def softmax_step(s_ref, p_ref, width, bias, causal, old_state, new_state, values, row_block):
    m_old, l_old, acc_old = old_state
    m_ref, l_ref, acc_ref = new_state
    total = s_ref.shape[0]
    for r in range(0, total, row_block):
        rows = slice(r, r + row_block)
        if causal is None:
            scores = s_ref[rows, 0:width] + bias
        else:
            plain = bias.shape[1]
            scores = jnp.concatenate([s_ref[rows, 0:plain] + bias, s_ref[rows, plain:width] + causal(r, row_block)], axis=1)
        peak = jnp.max(scores, axis=1, keepdims=True)
        if m_old is None:
            peak = jnp.broadcast_to(peak, (row_block, LANES))
        else:
            peak = jnp.maximum(m_old[rows, :], peak)
        powers = jnp.exp2((scores - jnp.concatenate([peak] * (width // LANES), axis=1)) * exp2_scale)
        added = jnp.sum(powers, axis=1, keepdims=True)
        if m_old is None:
            l_ref[rows, :] = jnp.broadcast_to(added, (row_block, LANES))
        else:
            factor = jnp.exp2((m_old[rows, :] - peak) * exp2_scale)
            l_ref[rows, :] = l_old[rows, :] * factor + added
            acc_ref[rows, :] = acc_old[rows, :] * jnp.concatenate([factor] * (LATENT_WIDTH // LANES), axis=1)
        m_ref[rows, :] = peak
        p_ref[rows, 0:width] = powers.astype(bf16)
    add = jnp.dot(p_ref[:, 0:width], values, preferred_element_type=f32)
    if m_old is None:
        acc_ref[...] = add
    else:
        acc_ref[...] += add


def state_shapes(total):
    stat = jax.ShapeDtypeStruct((total, LANES), f32)
    return [stat, stat, jax.ShapeDtypeStruct((total, LATENT_WIDTH), f32)]


def collect_suffix(key_ref, came, orders, page_width, share):
    core, member = lax.axis_index("tp"), lax.axis_index("dp") % TEAM
    half = came[0].shape[0] // 2
    for b in range(TEAM):
        rows = slice((b % 2) * half, (b % 2) * half + share)
        mine, theirs = came[b // 2][rows, page_width:], came[4 + b // 2][rows, page_width:]
        for side in range(2):
            piece = jnp.where(core == side, mine, theirs)
            source = member ^ sum(orders[side][k] for k in range(3) if (b >> k) & 1)
            at = pl.ds(pl.multiple_of(source * share, share), share)
            if side == 0:
                key_ref[at, 0:SUFFIX_LANES] = piece
            else:
                key_ref[at, SUFFIX_LANES:PADDED] = piece[:, 0 : PADDED - SUFFIX_LANES]


def attend(state, qe, qo, parts, page_width, row_block, suffix_len, tokens, suffix=None, last=None):
    n = len(parts)
    total = qe.shape[0]
    first = state is None
    per = page_width // WIDTH
    pieces = []
    for k, (page, _, _) in enumerate(parts):
        step = min(page.shape[0], CHUNK // 2)
        pieces += [(k, at, step) for at in range(0, page.shape[0], step)]
    groups, size = [[]], 0
    for piece in pieces:
        if size + piece[2] > CHUNK:
            groups.append([])
            size = 0
        groups[-1].append(piece)
        size += piece[2]
    widest = max(sum(p[2] for p in g) for g in groups) * per + (tokens if suffix else 0)
    n_came = 8 if suffix else 0

    def body(len_ref, qe_ref, qo_ref, *refs):
        page_refs, bias_refs, refs = refs[:n], refs[n : 2 * n], refs[2 * n :]
        came, refs = refs[:n_came], refs[n_came:]
        old = (None, None, None)
        if not first:
            old, refs = tuple(refs[:3]), refs[3:]
        if last:
            out_ref, refs = refs[0], refs[1:]
        new = tuple(refs[:3])
        s_ref, p_ref = refs[3:5]
        length = len_ref[lax.axis_index("dp") // TEAM]
        for number, group in enumerate(groups):
            evens, odds, ropes, even_bias, odd_bias = [], [], [], [], []
            for k, at, step in group:
                even, odd, rope = stack_keys(page_refs[k], slice(at, at + step), page_width)
                evens.append(even)
                odds.append(odd)
                ropes.append(rope)
                row, half_keys = parts[k][2], step * per // 2
                even_bias.append(bias_refs[k][row : row + 1, at * per : at * per + half_keys])
                odd_bias.append(bias_refs[k][row : row + 1, at * per + half_keys : at * per + 2 * half_keys])
            rope = jnp.concatenate(ropes, axis=0)
            even, odd = jnp.concatenate(evens, axis=0), jnp.concatenate(odds, axis=0)
            width = even.shape[0]
            s_ref[:, 0:width] = dot_nt(qe_ref[...], jnp.concatenate([even, rope], axis=1))
            s_ref[:, width : 2 * width] = dot_nt(qo_ref[...], jnp.concatenate([odd, rope], axis=1))
            width *= 2
            values, causal = [even, odd], None
            if suffix and number == len(groups) - 1:
                key_ref = refs[5]
                collect_suffix(key_ref, came, suffix[1], page_width, tokens // TEAM)
                s_ref[:, width : width + tokens] = dot_nt(qe_ref[...], key_ref[...])
                width += tokens
                values.append(key_ref[:, 0:LATENT_WIDTH])

                def causal(r, count):
                    u = iota((count, tokens), 1)
                    t = (iota((count, tokens), 0) + r) % tokens
                    return jnp.where((u <= t) & (u < length), 0.0, masked_score)

            bias = jnp.concatenate(even_bias + odd_bias, axis=1)
            softmax_step(s_ref, p_ref, width, bias, causal, old, new, jnp.concatenate(values, axis=0), row_block)
            old = new
        if last:
            _, l_ref, acc_ref = new
            live = iota((tokens, LATENT_WIDTH), 0) < length
            for h in range(last):
                rows = slice(h * tokens, (h + 1) * tokens)
                share = 1.0 / l_ref[rows, :]
                out = acc_ref[rows, :] * jnp.concatenate([share] * (LATENT_WIDTH // LANES), axis=1)
                out_ref[:, h * LATENT_WIDTH : (h + 1) * LATENT_WIDTH] = jnp.where(live, out, 0.0).astype(bf16)

    pages = [p for p, _, _ in parts]
    biases = [b for _, b, _ in parts]
    came = list(suffix[0]) if suffix else []
    carried = [] if first else list(state)
    n_in = 2 + 2 * n + len(came) + len(carried)
    scratch = [pltpu.VMEM((total, widest), f32), pltpu.VMEM((total, widest), bf16)]
    if suffix:
        scratch.append(pltpu.VMEM((tokens, PADDED), bf16))
    mib = 12 + (sum(p.size * 2 for p in pages + came) >> 20)
    outs = state_shapes(total)
    if last:
        scratch = [pltpu.VMEM(x.shape, f32) for x in outs] + scratch
        outs = [jax.ShapeDtypeStruct((tokens, last * LATENT_WIDTH), bf16)]
    return call(body, 1, n_in, outs, mib, scratch_shapes=scratch)(suffix_len, qe, qo, *pages, *biases, *came, *carried)


def program(pool, page_holder, page_slot, suffix_latent_rows, prefill_queries, suffix_len, decode_queries, decode_len):
    ranks = lax.axis_size("dp")
    teams = ranks // TEAM
    pull = page_holder.shape[0]
    cap = (pull + ranks - 1) // ranks
    width = -(-ranks * cap // LANES) * LANES
    page_width = pool.shape[1]
    tokens = prefill_queries.shape[1]
    heads = prefill_queries.shape[2] // WIDTH
    share = suffix_latent_rows.shape[1] // WIDTH

    table = request_table(page_holder.reshape(1, -1), page_slot.reshape(1, -1), ranks, cap, width)
    step = 1
    while step < ranks:
        table = table + xperm(table, (step, step))
        step *= 2

    qe, qo = prepare(prefill_queries[0], heads)
    pool = pair_pool(pool)
    dq = decode_queries.reshape(decode_queries.shape[0], -1, WIDTH)
    decode_part = decode(decode_len, pool, dq)

    suffix = jnp.pad(suffix_latent_rows.reshape(share, WIDTH), ((0, 0), (0, 2 * SUFFIX_LANES - WIDTH)))

    block = TEAM * cap
    if block % 32 == 0:
        streams = [(j, block // 2) for j in range(teams)]
    else:
        streams = [(0, teams * block // 2)]
    orders = [((1, 2, 4), (2, 4, 1)), ((4, 2, 1), (1, 4, 2))]
    orders = [orders[n % 2] for n in range(len(streams))]
    sent = gather_pages(table, pool, suffix, streams, cap)
    masks_of = key_masks(table, streams, cap, orders, page_width // WIDTH)

    came = []
    for n, (base, half) in enumerate(streams):
        rows = sent[n]
        unit = min(block, half)
        pieces = []
        for at in range(0, half, unit):
            masks = tuple(TEAM * (base + (c * half + at) // block) for c in range(2))
            piece = rows[at : at + unit, :page_width] if half > unit else rows
            pieces.append(xperm(piece, masks) if any(masks) else piece)
        if half > unit:
            rows = jnp.concatenate([jnp.concatenate(pieces, axis=0), rows[:, page_width:]], axis=1)
        else:
            rows = pieces[0]
        masks = list(zip(*orders[n]))
        got = xperm(rows, masks[0])
        both = jnp.concatenate([rows, got], axis=0)
        second = xperm(both, masks[1])
        third = xperm(both, masks[2])
        fourth = xperm(second, masks[2])
        own = [both, second, third, fourth]
        other = []
        for piece in own:
            other.append(sibling(piece))
        came.append((own, other))

    row_block = 128
    plan = []
    for n in range(len(streams)):
        own, other = came[n]
        piece = [[(own[k], masks_of[n], k), (other[k], masks_of[n], 4 + k)] for k in range(4)]
        plan.append((f"att{n}a", piece[0] + piece[1]))
        if n < len(streams) - 1:
            plan.append((f"att{n}b", piece[2] + piece[3]))
        else:
            plan.append((f"att{n}b", piece[2]))
            plan.append((f"att{n}c", piece[3]))
    tail = "att0b" if len(streams) > 1 else plan[-1][0]
    state = None
    for n, (name, group) in enumerate(plan):
        suffix = (came[0][0] + came[0][1], orders[0]) if name == tail else None
        last = heads if n == len(plan) - 1 else None
        state = attend(state, qe, qo, group, page_width, row_block, suffix_len, tokens, suffix, last)
    return (state[None], decode_part)


def solution(mesh):
    placed = (
        P(("groups", "dp"), None),
        P(("groups", "dp")),
        P(("groups", "dp")),
        P(("groups", "dp"), None),
        P(("groups", "dp"), None, "tp"),
        P("groups"),
        P(("groups", "dp"), "tp"),
        P(("groups", "dp")),
    )
    return jax.shard_map(
        program,
        mesh=mesh,
        in_specs=placed,
        out_specs=(P(("groups", "dp"), None, "tp"), P(("groups", "dp"), "tp")),
        check_vma=False,
    )
```

profile of v0, /device:TPU:0, one launch (start us, length us, event | category | flops | bytes accessed | tf_op | source)
XLA Modules:
  0.0 71.9 jit_solution(1452498959504056270)
XLA Ops:
  2.2 3.0 %collective-permute-start = (s32[16,128]{1,0:T(8,128)S(1)}, s32[16,128]{1,0:T(8,128)S(1)}, u32[]{:S(2)}, u32[]{:S(2)}) collective-permute-start(s32[16,128]{1,0:T(8,128)S(1)} %shard_map.96), channel_id=1, source_target_pairs={{0,2},{1,3},{2,0},{3,1},{4,6},{5,7},{6,4},{7,5},{8,10},{9,11},{10,... | collective-permute-start | bytes 24584 | tf_op jit(solution)/shard_map/ppermute | solution.py:56
  5.2 1.6 %collective-permute-done = s32[16,128]{1,0:T(8,128)S(1)} collective-permute-done((s32[16,128]{1,0:T(8,128)S(1)}, s32[16,128]{1,0:T(8,128)S(1)}, u32[]{:S(2)}, u32[]{:S(2)}) %collective-permute-start) | collective-permute-done | bytes 8224 | tf_op jit(solution)/shard_map/ppermute | solution.py:56
  6.8 2.0 %collective-permute-start.1 = (s32[16,128]{1,0:T(8,128)S(1)}, s32[16,128]{1,0:T(8,128)S(1)}, u32[]{:S(2)}, u32[]{:S(2)}) collective-permute-start(s32[16,128]{1,0:T(8,128)S(1)} %add.14), channel_id=1, source_target_pairs={{0,4},{1,5},{2,6},{3,7},{4,0},{5,1},{6,2},{7,3},{8,12},{9,13},{10,... | collective-permute-start | bytes 24584 | tf_op jit(solution)/shard_map/ppermute | solution.py:56
  8.9 1.6 %collective-permute-done.1 = s32[16,128]{1,0:T(8,128)S(1)} collective-permute-done((s32[16,128]{1,0:T(8,128)S(1)}, s32[16,128]{1,0:T(8,128)S(1)}, u32[]{:S(2)}, u32[]{:S(2)}) %collective-permute-start.1) | collective-permute-done | bytes 8224 | tf_op jit(solution)/shard_map/ppermute | solution.py:56
  10.5 2.1 %collective-permute-start.2 = (s32[16,128]{1,0:T(8,128)S(1)}, s32[16,128]{1,0:T(8,128)S(1)}, u32[]{:S(2)}, u32[]{:S(2)}) collective-permute-start(s32[16,128]{1,0:T(8,128)S(1)} %add.15), channel_id=1, source_target_pairs={{0,8},{1,9},{2,10},{3,11},{4,12},{5,13},{6,14},{7,15},{8,0},{9,1},... | collective-permute-start | bytes 24584 | tf_op jit(solution)/shard_map/ppermute | solution.py:56
  12.6 1.6 %collective-permute-done.2 = s32[16,128]{1,0:T(8,128)S(1)} collective-permute-done((s32[16,128]{1,0:T(8,128)S(1)}, s32[16,128]{1,0:T(8,128)S(1)}, u32[]{:S(2)}, u32[]{:S(2)}) %collective-permute-start.2) | collective-permute-done | bytes 8224 | tf_op jit(solution)/shard_map/ppermute | solution.py:56
  14.2 3.0 %collective-permute-start.3 = (s32[16,128]{1,0:T(8,128)S(1)}, s32[16,128]{1,0:T(8,128)S(1)}, u32[]{:S(2)}, u32[]{:S(2)}) collective-permute-start(s32[16,128]{1,0:T(8,128)S(1)} %add.16), channel_id=1, source_target_pairs={{0,16},{1,17},{2,18},{3,19},{4,20},{5,21},{6,22},{7,23},{8,24},{9,... | collective-permute-start | bytes 24584 | tf_op jit(solution)/shard_map/ppermute | solution.py:56
  20.1 2.5 %collective-permute-start.4 = (bf16[16,4608]{1,0:T(8,128)(2,1)S(1)}, bf16[16,4608]{1,0:T(8,128)(2,1)S(1)}, u32[]{:S(2)}, u32[]{:S(2)}) collective-permute-start(bf16[16,4608]{1,0:T(8,128)(2,1)S(1)} %get-tuple-element.22), channel_id=1, source_target_pairs={{0,16},{1,17},{2,18},{3,19},{4,20},{5,21},{6,22},{7,23},{8,24},{9,... | collective-permute-start | bytes 442376 | tf_op jit(solution)/shard_map/ppermute | solution.py:56
  22.6 1.6 %collective-permute-start.13 = (bf16[16,4992]{1,0:T(8,128)(2,1)S(1)}, bf16[16,4992]{1,0:T(8,128)(2,1)S(1)}, u32[]{:S(2)}, u32[]{:S(2)}) collective-permute-start(bf16[16,4992]{1,0:T(8,128)(2,1)S(1)} %get-tuple-element.24), channel_id=1, source_target_pairs={{0,2},{1,5},{2,0},{3,7},{4,6},{5,1},{6,4},{7,3},{8,10},{9,13},{10,... | collective-permute-start | bytes 479240 | tf_op jit(solution)/shard_map/ppermute | solution.py:56
  24.1 2.1 %collective-permute-done.4 = bf16[16,4608]{1,0:T(8,128)(2,1)S(1)} collective-permute-done((bf16[16,4608]{1,0:T(8,128)(2,1)S(1)}, bf16[16,4608]{1,0:T(8,128)(2,1)S(1)}, u32[]{:S(2)}, u32[]{:S(2)}) %collective-permute-start.4) | collective-permute-done | bytes 147488 | tf_op jit(solution)/shard_map/ppermute | solution.py:56
  26.9 2.1 %collective-permute-start.5 = (bf16[16,4608]{1,0:T(8,128)(2,1)S(1)}, bf16[16,4608]{1,0:T(8,128)(2,1)S(1)}, u32[]{:S(2)}, u32[]{:S(2)}) collective-permute-start(bf16[16,4608]{1,0:T(8,128)(2,1)S(1)} %collective-permute-done.4), channel_id=1, source_target_pairs={{0,8},{1,3},{2,10},{3,1},{4,12},{5,7},{6,14},{7,5},{8,0},{9,11},{1... | collective-permute-start | bytes 442376 | tf_op jit(solution)/shard_map/ppermute | solution.py:56
  29.5 1.6 %collective-permute-start.16 = (bf16[32,4992]{1,0:T(8,128)(2,1)S(1)}, bf16[32,4992]{1,0:T(8,128)(2,1)S(1)}, u32[]{:S(2)}, u32[]{:S(2)}) collective-permute-start(bf16[32,4992]{1,0:T(8,128)(2,1)S(1)} %constant_dynamic-update-slice_fusion.2.refs_0_.refs_8_), channel_id=1, source_target_pairs={{0,4},{1,9},{2,6},{3,11},{4,0},{5,13},{6,2},{7,15},{8,12},{9,1},{1... | collective-permute-start | bytes 958472 | tf_op jit(solution)/shard_map/ppermute | solution.py:56
  33.1 1.5 %collective-permute-start.6 = (bf16[32,4608]{1,0:T(8,128)(2,1)}, bf16[32,4608]{1,0:T(8,128)(2,1)}, u32[]{:S(2)}, u32[]{:S(2)}) collective-permute-start(bf16[32,4608]{1,0:T(8,128)(2,1)} %constant_dynamic-update-slice_fusion.refs_0_), channel_id=1, source_target_pairs={{0,4},{1,9},{2,6},{3,11},{4,0},{5,13},{6,2},{7,15},{8,12},{9,1},{1... | collective-permute-start | bytes 884744 | tf_op jit(solution)/shard_map/ppermute | solution.py:56
  34.6 1.9 %collective-permute-done.16.refs_2_.refs_9_ = bf16[32,4992]{1,0:T(8,128)(2,1)S(1)} collective-permute-done((bf16[32,4992]{1,0:T(8,128)(2,1)S(1)}, bf16[32,4992]{1,0:T(8,128)(2,1)S(1)}, u32[]{:S(2)}, u32[]{:S(2)}) %collective-permute-start.16) | collective-permute-done | bytes 319520 | tf_op jit(solution)/shard_map/ppermute | solution.py:56
  37.6 2.2 %collective-permute-done.14.refs_0_.refs_10_ = bf16[32,4992]{1,0:T(8,128)(2,1)S(1)} collective-permute-done((bf16[32,4992]{1,0:T(8,128)(2,1)S(1)}, bf16[32,4992]{1,0:T(8,128)(2,1)S(1)}, u32[]{:S(2)}, u32[]{:S(2)}) %collective-permute-start.14) | collective-permute-done | bytes 319520 | tf_op jit(solution)/shard_map/ppermute | solution.py:56
  40.5 2.6 %collective-permute-start.9 = (bf16[32,4608]{1,0:T(8,128)(2,1)}, bf16[32,4608]{1,0:T(8,128)(2,1)}, u32[]{:S(2)}, u32[]{:S(2)}) collective-permute-start(bf16[32,4608]{1,0:T(8,128)(2,1)} %constant_dynamic-update-slice_fusion.refs_0_), channel_id=1, source_target_pairs={{0,2},{1,5},{2,0},{3,7},{4,6},{5,1},{6,4},{7,3},{8,10},{9,13},{10,... | collective-permute-start | bytes 884744 | tf_op jit(solution)/shard_map/ppermute | solution.py:56
  44.7 3.4 %collective-permute-done.9.refs_0_ = bf16[32,4608]{1,0:T(8,128)(2,1)} collective-permute-done((bf16[32,4608]{1,0:T(8,128)(2,1)}, bf16[32,4608]{1,0:T(8,128)(2,1)}, u32[]{:S(2)}, u32[]{:S(2)}) %collective-permute-start.9) | collective-permute-done | bytes 294944 | tf_op jit(solution)/shard_map/ppermute | solution.py:56
  51.5 1.8 %reshape.19.q_ref = bf16[4,32,576]{2,1,0:T(8,128)(2,1)} reshape(bf16[4,18432]{1,0:T(4,128)(2,1)} %param.14) | data formatting | bytes 294912 | tf_op jit(solution)/shard_map/reshape | solution.py:433
  54.2 2.8 %shard_map.105 = bf16[4,16384]{1,0:T(4,128)(2,1)} custom-call(s32[4]{0:T(128)S(1)} %copy-done.10, bf16[128,4608]{1,0:T(8,128)(2,1)S(1)} %shard_map.97.pool_ref, bf16[4,32,576]{2,1,0:T(8,128)(2,1)S(1)} %copy-done.7), custom_call_target="tpu_custom_call" | custom-call | tf_op jit(solution)/shard_map/pallas_call | solution.py:182
  57.4 2.4 %shard_map.100 = (f32[512,128]{1,0:T(8,128)S(1)}, f32[512,128]{1,0:T(8,128)S(1)}, f32[512,512]{1,0:T(8,128)S(1)}) custom-call(s32[2]{0:T(128)S(1)} %copy-done.9, bf16[512,640]{1,0:T(8,128)(2,1)S(1)} %get-tuple-element.20.qe_ref, bf16[512,640]{1,0:T(8,128)(2,1)S(1)} %get-tuple-element.21.qo_ref, ...), custom_call_target="tpu_custom_call" | custom-call | tf_op jit(solution)/shard_map/pallas_call | solution.py:411
  59.8 3.8 %shard_map.101 = (f32[512,128]{1,0:T(8,128)S(1)}, f32[512,128]{1,0:T(8,128)S(1)}, f32[512,512]{1,0:T(8,128)S(1)}) custom-call(s32[2]{0:T(128)S(1)} %copy-done.9, bf16[512,640]{1,0:T(8,128)(2,1)S(1)} %get-tuple-element.20.qe_ref, bf16[512,640]{1,0:T(8,128)(2,1)S(1)} %get-tuple-element.21.qo_ref, bf16[32,4992]{1,0:T(8,128)(2,1)S(1)} %copy-done.1, ...), custom_call_target="tpu_custom_call" | custom-call | tf_op jit(solution)/shard_map/pallas_call | solution.py:411
  63.6 3.2 %shard_map.102 = (f32[512,128]{1,0:T(8,128)S(1)}, f32[512,128]{1,0:T(8,128)S(1)}, f32[512,512]{1,0:T(8,128)S(1)}) custom-call(s32[2]{0:T(128)S(1)} %copy-done.9, bf16[512,640]{1,0:T(8,128)(2,1)S(1)} %get-tuple-element.20.qe_ref, bf16[512,640]{1,0:T(8,128)(2,1)S(1)} %get-tuple-element.21.qo_ref, bf16[32,4608]{1,0:T(8,128)(2,1)} %constant_dynamic-update-slice_fusion.refs_0_, ...), custom_call_target="tpu_custom_call" | custom-call | tf_op jit(solution)/shard_map/pallas_call | solution.py:411
  66.8 2.1 %shard_map.103 = (f32[512,128]{1,0:T(8,128)S(1)}, f32[512,128]{1,0:T(8,128)S(1)}, f32[512,512]{1,0:T(8,128)S(1)}) custom-call(s32[2]{0:T(128)S(1)} %copy-done.9, bf16[512,640]{1,0:T(8,128)(2,1)S(1)} %get-tuple-element.20.qe_ref, bf16[512,640]{1,0:T(8,128)(2,1)S(1)} %get-tuple-element.21.qo_ref, bf16[32,4608]{1,0:T(8,128)(2,1)} %collective-permute-done.9.refs_0_, ...), custom_call_target="tpu_custom_call" | custom-call | tf_op jit(solution)/shard_map/pallas_call | solution.py:411
  68.9 2.9 %shard_map.104 = bf16[128,2048]{1,0:T(8,128)(2,1)} custom-call(s32[2]{0:T(128)S(1)} %copy-done.9, bf16[512,640]{1,0:T(8,128)(2,1)S(1)} %get-tuple-element.20.qe_ref, bf16[512,640]{1,0:T(8,128)(2,1)S(1)} %get-tuple-element.21.qo_ref, bf16[32,4608]{1,0:T(8,128)(2,1)} %collective-permute-done.7.refs_0_, bf16[32,4608]{1,0:T(8,128)(2,1)} %collective-permute-done.8.refs_1_, ...), custom_call_target="tpu_custom_call" | custom-call | tf_op jit(solution)/shard_map/pallas_call | solution.py:411
  (69 shorter events, 15.4 us)
Async XLA Ops:
  2.2 4.7 %collective-permute-start = (s32[16,128]{1,0:T(8,128)S(1)}, s32[16,128]{1,0:T(8,128)S(1)}, u32[]{:S(2)}, u32[]{:S(2)}) collective-permute-start(s32[16,128]{1,0:T(8,128)S(1)} %shard_map.96), channel_id=1, source_target_pairs={{0,2},{1,3},{2,0},{3,1},{4,6},{5,7},{6,4},{7,5},{8,10},{9,11},{10,... | collective-permute-start | bytes 24584 | tf_op jit(solution)/shard_map/ppermute | solution.py:56
  6.8 3.7 %collective-permute-start.1 = (s32[16,128]{1,0:T(8,128)S(1)}, s32[16,128]{1,0:T(8,128)S(1)}, u32[]{:S(2)}, u32[]{:S(2)}) collective-permute-start(s32[16,128]{1,0:T(8,128)S(1)} %add.14), channel_id=1, source_target_pairs={{0,4},{1,5},{2,6},{3,7},{4,0},{5,1},{6,2},{7,3},{8,12},{9,13},{10,... | collective-permute-start | bytes 24584 | tf_op jit(solution)/shard_map/ppermute | solution.py:56
  10.5 3.7 %collective-permute-start.2 = (s32[16,128]{1,0:T(8,128)S(1)}, s32[16,128]{1,0:T(8,128)S(1)}, u32[]{:S(2)}, u32[]{:S(2)}) collective-permute-start(s32[16,128]{1,0:T(8,128)S(1)} %add.15), channel_id=1, source_target_pairs={{0,8},{1,9},{2,10},{3,11},{4,12},{5,13},{6,14},{7,15},{8,0},{9,1},... | collective-permute-start | bytes 24584 | tf_op jit(solution)/shard_map/ppermute | solution.py:56
  14.2 5.3 %collective-permute-start.3 = (s32[16,128]{1,0:T(8,128)S(1)}, s32[16,128]{1,0:T(8,128)S(1)}, u32[]{:S(2)}, u32[]{:S(2)}) collective-permute-start(s32[16,128]{1,0:T(8,128)S(1)} %add.16), channel_id=1, source_target_pairs={{0,16},{1,17},{2,18},{3,19},{4,20},{5,21},{6,22},{7,23},{8,24},{9,... | collective-permute-start | bytes 24584 | tf_op jit(solution)/shard_map/ppermute | solution.py:56
  19.5 31.8 %copy-start.8 = (bf16[1,128,2304]{2,1,0:T(8,128)(2,1)S(1)}, bf16[1,128,2304]{2,1,0:T(8,128)(2,1)}, u32[]{:S(2)}) copy-start(bf16[1,128,2304]{2,1,0:T(8,128)(2,1)} %param.12) | copy-start | bytes 1769476
  20.1 33.2 %copy-start.10 = (s32[4]{0:T(128)S(1)}, s32[4]{0:T(128)}, u32[]{:S(2)}) copy-start(s32[4]{0:T(128)} %len_ref.11) | copy-start | bytes 52
  20.1 6.1 %collective-permute-start.4 = (bf16[16,4608]{1,0:T(8,128)(2,1)S(1)}, bf16[16,4608]{1,0:T(8,128)(2,1)S(1)}, u32[]{:S(2)}, u32[]{:S(2)}) collective-permute-start(bf16[16,4608]{1,0:T(8,128)(2,1)S(1)} %get-tuple-element.22), channel_id=1, source_target_pairs={{0,16},{1,17},{2,18},{3,19},{4,20},{5,21},{6,22},{7,23},{8,24},{9,... | collective-permute-start | bytes 442376 | tf_op jit(solution)/shard_map/ppermute | solution.py:56
  22.6 6.9 %collective-permute-start.13 = (bf16[16,4992]{1,0:T(8,128)(2,1)S(1)}, bf16[16,4992]{1,0:T(8,128)(2,1)S(1)}, u32[]{:S(2)}, u32[]{:S(2)}) collective-permute-start(bf16[16,4992]{1,0:T(8,128)(2,1)S(1)} %get-tuple-element.24), channel_id=1, source_target_pairs={{0,2},{1,5},{2,0},{3,7},{4,6},{5,1},{6,4},{7,3},{8,10},{9,13},{10,... | collective-permute-start | bytes 479240 | tf_op jit(solution)/shard_map/ppermute | solution.py:56
  26.9 5.6 %collective-permute-start.5 = (bf16[16,4608]{1,0:T(8,128)(2,1)S(1)}, bf16[16,4608]{1,0:T(8,128)(2,1)S(1)}, u32[]{:S(2)}, u32[]{:S(2)}) collective-permute-start(bf16[16,4608]{1,0:T(8,128)(2,1)S(1)} %collective-permute-done.4), channel_id=1, source_target_pairs={{0,8},{1,3},{2,10},{3,1},{4,12},{5,7},{6,14},{7,5},{8,0},{9,11},{1... | collective-permute-start | bytes 442376 | tf_op jit(solution)/shard_map/ppermute | solution.py:56
  29.5 7.1 %collective-permute-start.16 = (bf16[32,4992]{1,0:T(8,128)(2,1)S(1)}, bf16[32,4992]{1,0:T(8,128)(2,1)S(1)}, u32[]{:S(2)}, u32[]{:S(2)}) collective-permute-start(bf16[32,4992]{1,0:T(8,128)(2,1)S(1)} %constant_dynamic-update-slice_fusion.2.refs_0_.refs_8_), channel_id=1, source_target_pairs={{0,4},{1,9},{2,6},{3,11},{4,0},{5,13},{6,2},{7,15},{8,12},{9,1},{1... | collective-permute-start | bytes 958472 | tf_op jit(solution)/shard_map/ppermute | solution.py:56
  31.0 9.5 %collective-permute-start.19 = (bf16[32,4992]{1,0:T(8,128)(2,1)S(1)}, bf16[32,4992]{1,0:T(8,128)(2,1)S(1)}, u32[]{:S(2)}, u32[]{:S(2)}) collective-permute-start(bf16[32,4992]{1,0:T(8,128)(2,1)S(1)} %constant_dynamic-update-slice_fusion.2.refs_0_.refs_8_), channel_id=1, source_target_pairs={{0,1},{1,0},{2,3},{3,2},{4,5},{5,4},{6,7},{7,6},{8,9},{9,8},{10,11... | collective-permute-start | bytes 958472 | tf_op jit(solution)/shard_map/ppermute | solution.py:60
  31.0 8.7 %collective-permute-start.14 = (bf16[32,4992]{1,0:T(8,128)(2,1)S(1)}, bf16[32,4992]{1,0:T(8,128)(2,1)S(1)}, u32[]{:S(2)}, u32[]{:S(2)}) collective-permute-start(bf16[32,4992]{1,0:T(8,128)(2,1)S(1)} %constant_dynamic-update-slice_fusion.2.refs_0_.refs_8_), channel_id=1, source_target_pairs={{0,8},{1,3},{2,10},{3,1},{4,12},{5,7},{6,14},{7,5},{8,0},{9,11},{1... | collective-permute-start | bytes 958472 | tf_op jit(solution)/shard_map/ppermute | solution.py:56
  33.1 10.0 %collective-permute-start.6 = (bf16[32,4608]{1,0:T(8,128)(2,1)}, bf16[32,4608]{1,0:T(8,128)(2,1)}, u32[]{:S(2)}, u32[]{:S(2)}) collective-permute-start(bf16[32,4608]{1,0:T(8,128)(2,1)} %constant_dynamic-update-slice_fusion.refs_0_), channel_id=1, source_target_pairs={{0,4},{1,9},{2,6},{3,11},{4,0},{5,13},{6,2},{7,15},{8,12},{9,1},{1... | collective-permute-start | bytes 884744 | tf_op jit(solution)/shard_map/ppermute | solution.py:56
  36.5 8.2 %collective-permute-start.17 = (bf16[32,4992]{1,0:T(8,128)(2,1)S(1)}, bf16[32,4992]{1,0:T(8,128)(2,1)}, u32[]{:S(2)}, u32[]{:S(2)}) collective-permute-start(bf16[32,4992]{1,0:T(8,128)(2,1)S(1)} %collective-permute-done.16.refs_2_.refs_9_), channel_id=1, source_target_pairs={{0,8},{1,3},{2,10},{3,1},{4,12},{5,7},{6,14},{7,5},{8,0},{9,11},{1... | collective-permute-start | bytes 958472 | tf_op jit(solution)/shard_map/ppermute | solution.py:56
  37.6 10.6 %collective-permute-start.20 = (bf16[32,4992]{1,0:T(8,128)(2,1)S(1)}, bf16[32,4992]{1,0:T(8,128)(2,1)S(1)}, u32[]{:S(2)}, u32[]{:S(2)}) collective-permute-start(bf16[32,4992]{1,0:T(8,128)(2,1)S(1)} %collective-permute-done.16.refs_2_.refs_9_), channel_id=1, source_target_pairs={{0,1},{1,0},{2,3},{3,2},{4,5},{5,4},{6,7},{7,6},{8,9},{9,8},{10,11... | collective-permute-start | bytes 958472 | tf_op jit(solution)/shard_map/ppermute | solution.py:60
  39.8 9.6 %collective-permute-start.15 = (bf16[32,4992]{1,0:T(8,128)(2,1)S(1)}, bf16[32,4992]{1,0:T(8,128)(2,1)S(1)}, u32[]{:S(2)}, u32[]{:S(2)}) collective-permute-start(bf16[32,4992]{1,0:T(8,128)(2,1)S(1)} %collective-permute-done.14.refs_0_.refs_10_), channel_id=1, source_target_pairs={{0,1},{1,0},{2,3},{3,2},{4,5},{5,4},{6,7},{7,6},{8,9},{9,8},{10,11... | collective-permute-start | bytes 958472 | tf_op jit(solution)/shard_map/ppermute | solution.py:60
  40.5 7.7 %collective-permute-start.9 = (bf16[32,4608]{1,0:T(8,128)(2,1)}, bf16[32,4608]{1,0:T(8,128)(2,1)}, u32[]{:S(2)}, u32[]{:S(2)}) collective-permute-start(bf16[32,4608]{1,0:T(8,128)(2,1)} %constant_dynamic-update-slice_fusion.refs_0_), channel_id=1, source_target_pairs={{0,2},{1,5},{2,0},{3,7},{4,6},{5,1},{6,4},{7,3},{8,10},{9,13},{10,... | collective-permute-start | bytes 884744 | tf_op jit(solution)/shard_map/ppermute | solution.py:56
  43.1 8.2 %collective-permute-start.7 = (bf16[32,4608]{1,0:T(8,128)(2,1)}, bf16[32,4608]{1,0:T(8,128)(2,1)}, u32[]{:S(2)}, u32[]{:S(2)}) collective-permute-start(bf16[32,4608]{1,0:T(8,128)(2,1)} %collective-permute-done.6.refs_2_), channel_id=1, source_target_pairs={{0,2},{1,5},{2,0},{3,7},{4,6},{5,1},{6,4},{7,3},{8,10},{9,13},{10,... | collective-permute-start | bytes 884744 | tf_op jit(solution)/shard_map/ppermute | solution.py:56
  44.7 15.0 %collective-permute-start.18 = (bf16[32,4992]{1,0:T(8,128)(2,1)}, bf16[32,4992]{1,0:T(8,128)(2,1)}, u32[]{:S(2)}, u32[]{:S(2)}) collective-permute-start(bf16[32,4992]{1,0:T(8,128)(2,1)} %collective-permute-done.17.refs_2_.refs_11_), channel_id=1, source_target_pairs={{0,1},{1,0},{2,3},{3,2},{4,5},{5,4},{6,7},{7,6},{8,9},{9,8},{10,11... | collective-permute-start | bytes 958472 | tf_op jit(solution)/shard_map/ppermute | solution.py:60
  48.2 15.5 %collective-permute-start.11 = (bf16[32,4608]{1,0:T(8,128)(2,1)}, bf16[32,4608]{1,0:T(8,128)(2,1)}, u32[]{:S(2)}, u32[]{:S(2)}) collective-permute-start(bf16[32,4608]{1,0:T(8,128)(2,1)} %constant_dynamic-update-slice_fusion.refs_0_), channel_id=1, source_target_pairs={{0,1},{1,0},{2,3},{3,2},{4,5},{5,4},{6,7},{7,6},{8,9},{9,8},{10,11... | collective-permute-start | bytes 884744 | tf_op jit(solution)/shard_map/ppermute | solution.py:60
  48.9 14.7 %collective-permute-start.12 = (bf16[32,4608]{1,0:T(8,128)(2,1)}, bf16[32,4608]{1,0:T(8,128)(2,1)}, u32[]{:S(2)}, u32[]{:S(2)}) collective-permute-start(bf16[32,4608]{1,0:T(8,128)(2,1)} %collective-permute-done.6.refs_2_), channel_id=1, source_target_pairs={{0,1},{1,0},{2,3},{3,2},{4,5},{5,4},{6,7},{7,6},{8,9},{9,8},{10,11... | collective-permute-start | bytes 884744 | tf_op jit(solution)/shard_map/ppermute | solution.py:60
  50.1 16.7 %collective-permute-start.10 = (bf16[32,4608]{1,0:T(8,128)(2,1)}, bf16[32,4608]{1,0:T(8,128)(2,1)}, u32[]{:S(2)}, u32[]{:S(2)}) collective-permute-start(bf16[32,4608]{1,0:T(8,128)(2,1)} %collective-permute-done.9.refs_0_), channel_id=1, source_target_pairs={{0,1},{1,0},{2,3},{3,2},{4,5},{5,4},{6,7},{7,6},{8,9},{9,8},{10,11... | collective-permute-start | bytes 884744 | tf_op jit(solution)/shard_map/ppermute | solution.py:60
  51.3 17.6 %collective-permute-start.8 = (bf16[32,4608]{1,0:T(8,128)(2,1)}, bf16[32,4608]{1,0:T(8,128)(2,1)}, u32[]{:S(2)}, u32[]{:S(2)}) collective-permute-start(bf16[32,4608]{1,0:T(8,128)(2,1)} %collective-permute-done.7.refs_0_), channel_id=1, source_target_pairs={{0,1},{1,0},{2,3},{3,2},{4,5},{5,4},{6,7},{7,6},{8,9},{9,8},{10,11... | collective-permute-start | bytes 884744 | tf_op jit(solution)/shard_map/ppermute | solution.py:60
  51.3 6.0 %copy-start.9 = (s32[2]{0:T(128)S(1)}, s32[2]{0:T(128)}, u32[]{:S(2)}) copy-start(s32[2]{0:T(128)} %len_ref.10) | copy-start | bytes 28
  (11 other events, 14.4 us)
where the time goes:
time: 72.7 us; the launch traced here: 71.9 us
  starting transfers between devices  24.8 us (34%)
  Pallas kernels  18.7 us (26%)
  waiting for transfers between devices  18 us (25%)
  local copies, waits for them, and re-layouts  9.45 us (13%)
  between operations  0.87 us (1%)
    ppermute x13, starting transfers between devices, xperm(): return lax.ppermute(value, ('dp', 'tp'), pairs)  24.3 us
    ppermute x13, waiting for transfers between devices, xperm(): return lax.ppermute(value, ('dp', 'tp'), pairs)  18 us
    pallas_call x5, Pallas kernels, attend(): call(body, 1, n_in, outs, mib, scratch_shapes=scratch)  14.4 us
    unnamed x30, local copies, waits for them, and re-layouts  6.9 us
    pallas_call x1, Pallas kernels, decode(): call(body, 1, 2, [jax.ShapeDtypeStruct((rows, heads * LATENT_WIDTH), bf16)])  2.81 us
    reshape x1, local copies, waits for them, and re-layouts, program(): dq = decode_queries.reshape(decode_queries.shape[0], -1, WIDTH)  1.77 us
  transfers between devices with their start and end apart: 21, of which 11 were waited for; matrix products, arithmetic and copies ran while one was open for 5% of the time, Pallas kernels for 21%

commit v1 on v0

--- a/solution.py
+++ b/solution.py
@@ -60,20 +60,12 @@
     return lax.ppermute(value, "tp", [(0, 1), (1, 0)])
 
 
-def request_table(holder, slot, ranks, cap, width):
-    count = holder.shape[1]
-
-    def body(h_hbm, s_hbm, out_ref, h_ref, s_ref, sems):
-        copies = [
-            pltpu.make_async_copy(h_hbm, h_ref, sems.at[0]),
-            pltpu.make_async_copy(s_hbm, s_ref, sems.at[1]),
-        ]
-        for copy in copies:
-            copy.start()
-        for copy in copies:
-            copy.wait()
-        hrow = jnp.broadcast_to(h_ref[...], (count, count))
-        srow = jnp.broadcast_to(s_ref[...], (count, count))
+def request_table(asked, ranks, cap, width):
+    count = asked.shape[1]
+
+    def body(asked_ref, out_ref):
+        hrow = jnp.broadcast_to(asked_ref[0:1, :], (count, count))
+        srow = jnp.broadcast_to(asked_ref[1:2, :], (count, count))
         i, j = iota((count, count), 0), iota((count, count), 1)
         hcol = jnp.sum(jnp.where(i == j, hrow, 0), axis=1, keepdims=True)
         scol = jnp.sum(jnp.where(i == j, srow, 0), axis=1, keepdims=True)
@@ -83,18 +75,7 @@
         row = jnp.sum(hit, axis=0, keepdims=True)
         out_ref[...] = jnp.where(iota((ranks, width), 0) == lax.axis_index("dp"), row, 0)
 
-    return pl.pallas_call(
-        body,
-        in_specs=[pl.BlockSpec(memory_space=pltpu.HBM)] * 2,
-        out_specs=vmem(),
-        out_shape=jax.ShapeDtypeStruct((ranks, width), jnp.int32),
-        scratch_shapes=[
-            pltpu.VMEM((1, count), jnp.int32),
-            pltpu.VMEM((1, count), jnp.int32),
-            pltpu.SemaphoreType.DMA((2,)),
-        ],
-        compiler_params=pltpu.CompilerParams(vmem_limit_bytes=4 << 20),
-    )(holder, slot)
+    return call(body, 0, 1, [jax.ShapeDtypeStruct((ranks, width), jnp.int32)], 4)(asked)
 
 
 def paired(page, page_width):
@@ -188,7 +169,9 @@
     block = TEAM * cap
     total = sum(half for _, half in streams)
 
-    def body(table_ref, pool_ref, suffix_ref, *outs):
+    def body(table_ref, pool_ref, *outs):
+        if suffix is not None:
+            suffix_ref, outs = outs[0], outs[1:]
         me, core = lax.axis_index("dp"), lax.axis_index("tp")
         team = me // TEAM
         tab = table_ref[...].astype(f32).astype(bf16)
@@ -218,7 +201,7 @@
         for n, (_, half) in enumerate(streams):
             outs[n][:, 0:page_width] = rows[at : at + half]
             at += half
-            if n == 0:
+            if suffix is not None and n == 0:
                 left = suffix_ref[:, 0:SUFFIX_LANES]
                 right = suffix_ref[:, SUFFIX_LANES : 2 * SUFFIX_LANES]
                 if half > left.shape[0]:
@@ -226,10 +209,11 @@
                 outs[n][0 : left.shape[0], page_width:] = jnp.where(core == 0, left, right)
 
     outs = [
-        jax.ShapeDtypeStruct((half, page_width + (SUFFIX_LANES if n == 0 else 0)), bf16)
+        jax.ShapeDtypeStruct((half, page_width + (SUFFIX_LANES if n == 0 and suffix is not None else 0)), bf16)
         for n, (_, half) in enumerate(streams)
     ]
-    out = call(body, 0, 3, outs)(table, pool, suffix)
+    given = [table, pool] + ([] if suffix is None else [suffix])
+    out = call(body, 0, len(given), outs)(*given)
     return out if len(outs) > 1 else (out,)
 
 
@@ -403,7 +387,7 @@
     scratch = [pltpu.VMEM((total, widest), f32), pltpu.VMEM((total, widest), bf16)]
     if suffix:
         scratch.append(pltpu.VMEM((tokens, PADDED), bf16))
-    mib = 12 + (sum(p.size * 2 for p in pages + came) >> 20)
+    mib = 9 + (sum(p.size * 2 for p in pages + came) >> 20)
     outs = state_shapes(total)
     if last:
         scratch = [pltpu.VMEM(x.shape, f32) for x in outs] + scratch
@@ -422,27 +406,32 @@
     heads = prefill_queries.shape[2] // WIDTH
     share = suffix_latent_rows.shape[1] // WIDTH
 
-    table = request_table(page_holder.reshape(1, -1), page_slot.reshape(1, -1), ranks, cap, width)
+    table = request_table(jnp.stack([page_holder, page_slot]), ranks, cap, width)
+    block = TEAM * cap
+    split = block % 32 == 0
+    if split:
+        streams = [(j, block // 2) for j in range(teams)]
+    else:
+        streams = [(0, teams * block // 2)]
+    suffix = jnp.pad(suffix_latent_rows.reshape(share, WIDTH), ((0, 0), (0, 2 * SUFFIX_LANES - WIDTH)))
+    pool = pair_pool(pool)
+    sent = []
     step = 1
     while step < ranks:
         table = table + xperm(table, (step, step))
         step *= 2
-
+        if step == TEAM and split:
+            sent += gather_pages(table, pool, suffix, streams[:1], cap)
+    if split:
+        sent += gather_pages(table, pool, None, streams[1:], cap)
+    else:
+        sent += gather_pages(table, pool, suffix, streams, cap)
     qe, qo = prepare(prefill_queries[0], heads)
-    pool = pair_pool(pool)
     dq = decode_queries.reshape(decode_queries.shape[0], -1, WIDTH)
     decode_part = decode(decode_len, pool, dq)
 
-    suffix = jnp.pad(suffix_latent_rows.reshape(share, WIDTH), ((0, 0), (0, 2 * SUFFIX_LANES - WIDTH)))
-
-    block = TEAM * cap
-    if block % 32 == 0:
-        streams = [(j, block // 2) for j in range(teams)]
-    else:
-        streams = [(0, teams * block // 2)]
     orders = [((1, 2, 4), (2, 4, 1)), ((4, 2, 1), (1, 4, 2))]
     orders = [orders[n % 2] for n in range(len(streams))]
-    sent = gather_pages(table, pool, suffix, streams, cap)
     masks_of = key_masks(table, streams, cap, orders, page_width // WIDTH)
 
     came = []

time: 72.7 us -> 72 us (level)
  waiting for transfers between devices: 18 us -> 14.8 us
  starting transfers between devices: 24.8 us -> 27.8 us
  local copies, waits for them, and re-layouts: 9.45 us -> 7.61 us
    ppermute x13, waiting for transfers between devices: 18 us -> 14.8 us  [xperm(): return lax.ppermute(value, ('dp', 'tp'), pairs)]
    ppermute x13, starting transfers between devices: 24.3 us -> 27.3 us  [xperm(): return lax.ppermute(value, ('dp', 'tp'), pairs)]
    unnamed x30 -> x25, local copies, waits for them, and re-layouts: 6.9 us -> 5.07 us
  transfers between devices with their start and end apart: 21 -> 21, of which waited for: 11 -> 10; matrix products, arithmetic and copies ran while one was open for 5% -> 5% of each run, Pallas kernels for 21% -> 22%
where the time goes in v1:
time: 72 us; the launch traced here: 71 us
  starting transfers between devices  27.8 us (39%)
  Pallas kernels  19.1 us (27%)
  waiting for transfers between devices  14.8 us (21%)
  local copies, waits for them, and re-layouts  7.61 us (11%)
  between operations  0.83 us (1%)
  other arithmetic  0.82 us (1%)
    ppermute x13, starting transfers between devices, xperm(): return lax.ppermute(value, ('dp', 'tp'), pairs)  27.3 us
    ppermute x13, waiting for transfers between devices, xperm(): return lax.ppermute(value, ('dp', 'tp'), pairs)  14.8 us
    pallas_call x5, Pallas kernels, attend(): call(body, 1, n_in, outs, mib, scratch_shapes=scratch)  14.5 us
    unnamed x25, local copies, waits for them, and re-layouts  5.07 us
    pallas_call x1, Pallas kernels, decode(): call(body, 1, 2, [jax.ShapeDtypeStruct((rows, heads * LATENT_WIDTH), bf16)])  2.81 us
    reshape x1, local copies, waits for them, and re-layouts, program(): dq = decode_queries.reshape(decode_queries.shape[0], -1, WIDTH)  1.77 us
  transfers between devices with their start and end apart: 21, of which 10 were waited for; matrix products, arithmetic and copies ran while one was open for 5% of the time, Pallas kernels for 22%

profile of v1, /device:TPU:0, one launch (start us, length us, event | category | flops | bytes accessed | tf_op | source)
XLA Modules:
  0.0 71.0 jit_solution(3525329384130834679)
XLA Ops:
  1.5 3.0 %collective-permute-start = (s32[16,128]{1,0:T(8,128)S(1)}, s32[16,128]{1,0:T(8,128)S(1)}, u32[]{:S(2)}, u32[]{:S(2)}) collective-permute-start(s32[16,128]{1,0:T(8,128)S(1)} %shard_map.96), channel_id=1, source_target_pairs={{0,2},{1,3},{2,0},{3,1},{4,6},{5,7},{6,4},{7,5},{8,10},{9,11},{10,... | collective-permute-start | bytes 24584 | tf_op jit(solution)/shard_map/ppermute | solution.py:56
  4.5 1.6 %collective-permute-done = s32[16,128]{1,0:T(8,128)S(1)} collective-permute-done((s32[16,128]{1,0:T(8,128)S(1)}, s32[16,128]{1,0:T(8,128)S(1)}, u32[]{:S(2)}, u32[]{:S(2)}) %collective-permute-start) | collective-permute-done | bytes 8224 | tf_op jit(solution)/shard_map/ppermute | solution.py:56
  6.2 2.0 %collective-permute-start.1 = (s32[16,128]{1,0:T(8,128)S(1)}, s32[16,128]{1,0:T(8,128)S(1)}, u32[]{:S(2)}, u32[]{:S(2)}) collective-permute-start(s32[16,128]{1,0:T(8,128)S(1)} %add.14), channel_id=1, source_target_pairs={{0,4},{1,5},{2,6},{3,7},{4,0},{5,1},{6,2},{7,3},{8,12},{9,13},{10,... | collective-permute-start | bytes 24584 | tf_op jit(solution)/shard_map/ppermute | solution.py:56
  8.2 1.6 %collective-permute-done.1 = s32[16,128]{1,0:T(8,128)S(1)} collective-permute-done((s32[16,128]{1,0:T(8,128)S(1)}, s32[16,128]{1,0:T(8,128)S(1)}, u32[]{:S(2)}, u32[]{:S(2)}) %collective-permute-start.1) | collective-permute-done | bytes 8224 | tf_op jit(solution)/shard_map/ppermute | solution.py:56
  9.9 2.1 %collective-permute-start.2 = (s32[16,128]{1,0:T(8,128)S(1)}, s32[16,128]{1,0:T(8,128)S(1)}, u32[]{:S(2)}, u32[]{:S(2)}) collective-permute-start(s32[16,128]{1,0:T(8,128)S(1)} %add.15), channel_id=1, source_target_pairs={{0,8},{1,9},{2,10},{3,11},{4,12},{5,13},{6,14},{7,15},{8,0},{9,1},... | collective-permute-start | bytes 24584 | tf_op jit(solution)/shard_map/ppermute | solution.py:56
  11.9 1.6 %collective-permute-done.2 = s32[16,128]{1,0:T(8,128)S(1)} collective-permute-done((s32[16,128]{1,0:T(8,128)S(1)}, s32[16,128]{1,0:T(8,128)S(1)}, u32[]{:S(2)}, u32[]{:S(2)}) %collective-permute-start.2) | collective-permute-done | bytes 8224 | tf_op jit(solution)/shard_map/ppermute | solution.py:56
  13.6 3.0 %collective-permute-start.3 = (s32[16,128]{1,0:T(8,128)S(1)}, s32[16,128]{1,0:T(8,128)S(1)}, u32[]{:S(2)}, u32[]{:S(2)}) collective-permute-start(s32[16,128]{1,0:T(8,128)S(1)} %add.16.table_ref), channel_id=1, source_target_pairs={{0,16},{1,17},{2,18},{3,19},{4,20},{5,21},{6,22},{7,23},{8,24},{9,... | collective-permute-start | bytes 24584 | tf_op jit(solution)/shard_map/ppermute | solution.py:56
  18.7 3.1 %collective-permute-start.4 = (bf16[16,4608]{1,0:T(8,128)(2,1)S(1)}, bf16[16,4608]{1,0:T(8,128)(2,1)S(1)}, u32[]{:S(2)}, u32[]{:S(2)}) collective-permute-start(bf16[16,4608]{1,0:T(8,128)(2,1)S(1)} %shard_map.98), channel_id=1, source_target_pairs={{0,16},{1,17},{2,18},{3,19},{4,20},{5,21},{6,22},{7,23},{8,24},{9,... | collective-permute-start | bytes 442376 | tf_op jit(solution)/shard_map/ppermute | solution.py:56
  22.5 1.6 %collective-permute-start.13 = (bf16[16,4992]{1,0:T(8,128)(2,1)S(1)}, bf16[16,4992]{1,0:T(8,128)(2,1)S(1)}, u32[]{:S(2)}, u32[]{:S(2)}) collective-permute-start(bf16[16,4992]{1,0:T(8,128)(2,1)S(1)} %shard_map.100), channel_id=1, source_target_pairs={{0,2},{1,5},{2,0},{3,7},{4,6},{5,1},{6,4},{7,3},{8,10},{9,13},{10,... | collective-permute-start | bytes 479240 | tf_op jit(solution)/shard_map/ppermute | solution.py:56
  25.6 2.6 %collective-permute-start.5 = (bf16[16,4608]{1,0:T(8,128)(2,1)S(1)}, bf16[16,4608]{1,0:T(8,128)(2,1)S(1)}, u32[]{:S(2)}, u32[]{:S(2)}) collective-permute-start(bf16[16,4608]{1,0:T(8,128)(2,1)S(1)} %collective-permute-done.4), channel_id=1, source_target_pairs={{0,8},{1,3},{2,10},{3,1},{4,12},{5,7},{6,14},{7,5},{8,0},{9,11},{1... | collective-permute-start | bytes 442376 | tf_op jit(solution)/shard_map/ppermute | solution.py:56
  28.3 1.6 %collective-permute-start.16 = (bf16[32,4992]{1,0:T(8,128)(2,1)S(1)}, bf16[32,4992]{1,0:T(8,128)(2,1)S(1)}, u32[]{:S(2)}, u32[]{:S(2)}) collective-permute-start(bf16[32,4992]{1,0:T(8,128)(2,1)S(1)} %pad_maximum_fusion.refs_0_.refs_8_), channel_id=1, source_target_pairs={{0,4},{1,9},{2,6},{3,11},{4,0},{5,13},{6,2},{7,15},{8,12},{9,1},{1... | collective-permute-start | bytes 958472 | tf_op jit(solution)/shard_map/ppermute | solution.py:56
  29.9 2.1 %collective-permute-start.14 = (bf16[32,4992]{1,0:T(8,128)(2,1)S(1)}, bf16[32,4992]{1,0:T(8,128)(2,1)S(1)}, u32[]{:S(2)}, u32[]{:S(2)}) collective-permute-start(bf16[32,4992]{1,0:T(8,128)(2,1)S(1)} %pad_maximum_fusion.refs_0_.refs_8_), channel_id=1, source_target_pairs={{0,8},{1,3},{2,10},{3,1},{4,12},{5,7},{6,14},{7,5},{8,0},{9,11},{1... | collective-permute-start | bytes 958472 | tf_op jit(solution)/shard_map/ppermute | solution.py:56
  33.5 1.8 %collective-permute-done.16.refs_2_.refs_9_ = bf16[32,4992]{1,0:T(8,128)(2,1)S(1)} collective-permute-done((bf16[32,4992]{1,0:T(8,128)(2,1)S(1)}, bf16[32,4992]{1,0:T(8,128)(2,1)S(1)}, u32[]{:S(2)}, u32[]{:S(2)}) %collective-permute-start.16) | collective-permute-done | bytes 319520 | tf_op jit(solution)/shard_map/ppermute | solution.py:56
  35.3 2.1 %collective-permute-start.17 = (bf16[32,4992]{1,0:T(8,128)(2,1)S(1)}, bf16[32,4992]{1,0:T(8,128)(2,1)}, u32[]{:S(2)}, u32[]{:S(2)}) collective-permute-start(bf16[32,4992]{1,0:T(8,128)(2,1)S(1)} %collective-permute-done.16.refs_2_.refs_9_), channel_id=1, source_target_pairs={{0,8},{1,3},{2,10},{3,1},{4,12},{5,7},{6,14},{7,5},{8,0},{9,11},{1... | collective-permute-start | bytes 958472 | tf_op jit(solution)/shard_map/ppermute | solution.py:56
  39.2 3.0 %collective-permute-start.9 = (bf16[32,4608]{1,0:T(8,128)(2,1)}, bf16[32,4608]{1,0:T(8,128)(2,1)}, u32[]{:S(2)}, u32[]{:S(2)}) collective-permute-start(bf16[32,4608]{1,0:T(8,128)(2,1)} %constant_dynamic-update-slice_fusion.refs_0_), channel_id=1, source_target_pairs={{0,2},{1,5},{2,0},{3,7},{4,6},{5,1},{6,4},{7,3},{8,10},{9,13},{10,... | collective-permute-start | bytes 884744 | tf_op jit(solution)/shard_map/ppermute | solution.py:56
  42.3 1.3 %collective-permute-done.17.refs_2_.refs_11_ = bf16[32,4992]{1,0:T(8,128)(2,1)} collective-permute-done((bf16[32,4992]{1,0:T(8,128)(2,1)S(1)}, bf16[32,4992]{1,0:T(8,128)(2,1)}, u32[]{:S(2)}, u32[]{:S(2)}) %collective-permute-start.17) | collective-permute-done | bytes 319520 | tf_op jit(solution)/shard_map/ppermute | solution.py:56
  43.6 3.6 %collective-permute-done.9.refs_0_ = bf16[32,4608]{1,0:T(8,128)(2,1)} collective-permute-done((bf16[32,4608]{1,0:T(8,128)(2,1)}, bf16[32,4608]{1,0:T(8,128)(2,1)}, u32[]{:S(2)}, u32[]{:S(2)}) %collective-permute-start.9) | collective-permute-done | bytes 294944 | tf_op jit(solution)/shard_map/ppermute | solution.py:56
  50.6 1.8 %reshape.11.q_ref = bf16[4,32,576]{2,1,0:T(8,128)(2,1)} reshape(bf16[4,18432]{1,0:T(4,128)(2,1)} %param.14) | data formatting | bytes 294912 | tf_op jit(solution)/shard_map/reshape | solution.py:430
  53.3 2.8 %shard_map.106 = bf16[4,16384]{1,0:T(4,128)(2,1)} custom-call(s32[4]{0:T(128)S(1)} %copy-done.10, bf16[128,4608]{1,0:T(8,128)(2,1)S(1)} %shard_map.97.pool_ref, bf16[4,32,576]{2,1,0:T(8,128)(2,1)S(1)} %copy-done.7), custom_call_target="tpu_custom_call" | custom-call | tf_op jit(solution)/shard_map/pallas_call | solution.py:163
  56.4 2.4 %shard_map.101 = (f32[512,128]{1,0:T(8,128)S(1)}, f32[512,128]{1,0:T(8,128)S(1)}, f32[512,512]{1,0:T(8,128)S(1)}) custom-call(s32[2]{0:T(128)S(1)} %copy-done.9, bf16[512,640]{1,0:T(8,128)(2,1)S(1)} %get-tuple-element.18.qe_ref, bf16[512,640]{1,0:T(8,128)(2,1)S(1)} %get-tuple-element.19.qo_ref, bf16[32,4992]{1,0:T(8,128)(2,1)S(1)} %pad_maximum_fusion.refs_0_.refs_8_, ...), custom_call_target="tpu_custom_call" | custom-call | tf_op jit(solution)/shard_map/pallas_call | solution.py:395
  58.8 3.9 %shard_map.102 = (f32[512,128]{1,0:T(8,128)S(1)}, f32[512,128]{1,0:T(8,128)S(1)}, f32[512,512]{1,0:T(8,128)S(1)}) custom-call(s32[2]{0:T(128)S(1)} %copy-done.9, bf16[512,640]{1,0:T(8,128)(2,1)S(1)} %get-tuple-element.18.qe_ref, bf16[512,640]{1,0:T(8,128)(2,1)S(1)} %get-tuple-element.19.qo_ref, bf16[32,4992]{1,0:T(8,128)(2,1)S(1)} %copy-done.1, ...), custom_call_target="tpu_custom_call" | custom-call | tf_op jit(solution)/shard_map/pallas_call | solution.py:395
  62.7 3.2 %shard_map.103 = (f32[512,128]{1,0:T(8,128)S(1)}, f32[512,128]{1,0:T(8,128)S(1)}, f32[512,512]{1,0:T(8,128)S(1)}) custom-call(s32[2]{0:T(128)S(1)} %copy-done.9, bf16[512,640]{1,0:T(8,128)(2,1)S(1)} %get-tuple-element.18.qe_ref, bf16[512,640]{1,0:T(8,128)(2,1)S(1)} %get-tuple-element.19.qo_ref, bf16[32,4608]{1,0:T(8,128)(2,1)} %constant_dynamic-update-slice_fusion.refs_0_, ...), custom_call_target="tpu_custom_call" | custom-call | tf_op jit(solution)/shard_map/pallas_call | solution.py:395
  65.9 2.1 %shard_map.104 = (f32[512,128]{1,0:T(8,128)S(1)}, f32[512,128]{1,0:T(8,128)S(1)}, f32[512,512]{1,0:T(8,128)S(1)}) custom-call(s32[2]{0:T(128)S(1)} %copy-done.9, bf16[512,640]{1,0:T(8,128)(2,1)S(1)} %get-tuple-element.18.qe_ref, bf16[512,640]{1,0:T(8,128)(2,1)S(1)} %get-tuple-element.19.qo_ref, bf16[32,4608]{1,0:T(8,128)(2,1)} %collective-permute-done.9.refs_0_, ...), custom_call_target="tpu_custom_call" | custom-call | tf_op jit(solution)/shard_map/pallas_call | solution.py:395
  68.0 2.9 %shard_map.105 = bf16[128,2048]{1,0:T(8,128)(2,1)} custom-call(s32[2]{0:T(128)S(1)} %copy-done.9, bf16[512,640]{1,0:T(8,128)(2,1)S(1)} %get-tuple-element.18.qe_ref, bf16[512,640]{1,0:T(8,128)(2,1)S(1)} %get-tuple-element.19.qo_ref, bf16[32,4608]{1,0:T(8,128)(2,1)} %collective-permute-done.7.refs_0_, bf16[32,4608]{1,0:T(8,128)(2,1)} %collective-permute-done.8.refs_1_, ...), custom_call_target="tpu_custom_call" | custom-call | tf_op jit(solution)/shard_map/pallas_call | solution.py:395
  (66 shorter events, 13.1 us)
Async XLA Ops:
  1.5 4.7 %collective-permute-start = (s32[16,128]{1,0:T(8,128)S(1)}, s32[16,128]{1,0:T(8,128)S(1)}, u32[]{:S(2)}, u32[]{:S(2)}) collective-permute-start(s32[16,128]{1,0:T(8,128)S(1)} %shard_map.96), channel_id=1, source_target_pairs={{0,2},{1,3},{2,0},{3,1},{4,6},{5,7},{6,4},{7,5},{8,10},{9,11},{10,... | collective-permute-start | bytes 24584 | tf_op jit(solution)/shard_map/ppermute | solution.py:56
  6.2 3.7 %collective-permute-start.1 = (s32[16,128]{1,0:T(8,128)S(1)}, s32[16,128]{1,0:T(8,128)S(1)}, u32[]{:S(2)}, u32[]{:S(2)}) collective-permute-start(s32[16,128]{1,0:T(8,128)S(1)} %add.14), channel_id=1, source_target_pairs={{0,4},{1,5},{2,6},{3,7},{4,0},{5,1},{6,2},{7,3},{8,12},{9,13},{10,... | collective-permute-start | bytes 24584 | tf_op jit(solution)/shard_map/ppermute | solution.py:56
  9.9 3.7 %collective-permute-start.2 = (s32[16,128]{1,0:T(8,128)S(1)}, s32[16,128]{1,0:T(8,128)S(1)}, u32[]{:S(2)}, u32[]{:S(2)}) collective-permute-start(s32[16,128]{1,0:T(8,128)S(1)} %add.15), channel_id=1, source_target_pairs={{0,8},{1,9},{2,10},{3,11},{4,12},{5,13},{6,14},{7,15},{8,0},{9,1},... | collective-permute-start | bytes 24584 | tf_op jit(solution)/shard_map/ppermute | solution.py:56
  13.6 4.7 %collective-permute-start.3 = (s32[16,128]{1,0:T(8,128)S(1)}, s32[16,128]{1,0:T(8,128)S(1)}, u32[]{:S(2)}, u32[]{:S(2)}) collective-permute-start(s32[16,128]{1,0:T(8,128)S(1)} %add.16.table_ref), channel_id=1, source_target_pairs={{0,16},{1,17},{2,18},{3,19},{4,20},{5,21},{6,22},{7,23},{8,24},{9,... | collective-permute-start | bytes 24584 | tf_op jit(solution)/shard_map/ppermute | solution.py:56
  18.7 6.2 %collective-permute-start.4 = (bf16[16,4608]{1,0:T(8,128)(2,1)S(1)}, bf16[16,4608]{1,0:T(8,128)(2,1)S(1)}, u32[]{:S(2)}, u32[]{:S(2)}) collective-permute-start(bf16[16,4608]{1,0:T(8,128)(2,1)S(1)} %shard_map.98), channel_id=1, source_target_pairs={{0,16},{1,17},{2,18},{3,19},{4,20},{5,21},{6,22},{7,23},{8,24},{9,... | collective-permute-start | bytes 442376 | tf_op jit(solution)/shard_map/ppermute | solution.py:56
  22.0 28.4 %copy-start.8 = (bf16[1,128,2304]{2,1,0:T(8,128)(2,1)S(1)}, bf16[1,128,2304]{2,1,0:T(8,128)(2,1)}, u32[]{:S(2)}) copy-start(bf16[1,128,2304]{2,1,0:T(8,128)(2,1)} %param.12) | copy-start | bytes 1769476
  22.5 29.9 %copy-start.10 = (s32[4]{0:T(128)S(1)}, s32[4]{0:T(128)}, u32[]{:S(2)}) copy-start(s32[4]{0:T(128)} %len_ref.11) | copy-start | bytes 52
  22.5 5.7 %collective-permute-start.13 = (bf16[16,4992]{1,0:T(8,128)(2,1)S(1)}, bf16[16,4992]{1,0:T(8,128)(2,1)S(1)}, u32[]{:S(2)}, u32[]{:S(2)}) collective-permute-start(bf16[16,4992]{1,0:T(8,128)(2,1)S(1)} %shard_map.100), channel_id=1, source_target_pairs={{0,2},{1,5},{2,0},{3,7},{4,6},{5,1},{6,4},{7,3},{8,10},{9,13},{10,... | collective-permute-start | bytes 479240 | tf_op jit(solution)/shard_map/ppermute | solution.py:56
  25.6 6.4 %collective-permute-start.5 = (bf16[16,4608]{1,0:T(8,128)(2,1)S(1)}, bf16[16,4608]{1,0:T(8,128)(2,1)S(1)}, u32[]{:S(2)}, u32[]{:S(2)}) collective-permute-start(bf16[16,4608]{1,0:T(8,128)(2,1)S(1)} %collective-permute-done.4), channel_id=1, source_target_pairs={{0,8},{1,3},{2,10},{3,1},{4,12},{5,7},{6,14},{7,5},{8,0},{9,11},{1... | collective-permute-start | bytes 442376 | tf_op jit(solution)/shard_map/ppermute | solution.py:56
  28.3 7.1 %collective-permute-start.16 = (bf16[32,4992]{1,0:T(8,128)(2,1)S(1)}, bf16[32,4992]{1,0:T(8,128)(2,1)S(1)}, u32[]{:S(2)}, u32[]{:S(2)}) collective-permute-start(bf16[32,4992]{1,0:T(8,128)(2,1)S(1)} %pad_maximum_fusion.refs_0_.refs_8_), channel_id=1, source_target_pairs={{0,4},{1,9},{2,6},{3,11},{4,0},{5,13},{6,2},{7,15},{8,12},{9,1},{1... | collective-permute-start | bytes 958472 | tf_op jit(solution)/shard_map/ppermute | solution.py:56
  29.8 9.3 %collective-permute-start.19 = (bf16[32,4992]{1,0:T(8,128)(2,1)S(1)}, bf16[32,4992]{1,0:T(8,128)(2,1)S(1)}, u32[]{:S(2)}, u32[]{:S(2)}) collective-permute-start(bf16[32,4992]{1,0:T(8,128)(2,1)S(1)} %pad_maximum_fusion.refs_0_.refs_8_), channel_id=1, source_target_pairs={{0,1},{1,0},{2,3},{3,2},{4,5},{5,4},{6,7},{7,6},{8,9},{9,8},{10,11... | collective-permute-start | bytes 958472 | tf_op jit(solution)/shard_map/ppermute | solution.py:60
  29.9 8.6 %collective-permute-start.14 = (bf16[32,4992]{1,0:T(8,128)(2,1)S(1)}, bf16[32,4992]{1,0:T(8,128)(2,1)S(1)}, u32[]{:S(2)}, u32[]{:S(2)}) collective-permute-start(bf16[32,4992]{1,0:T(8,128)(2,1)S(1)} %pad_maximum_fusion.refs_0_.refs_8_), channel_id=1, source_target_pairs={{0,8},{1,3},{2,10},{3,1},{4,12},{5,7},{6,14},{7,5},{8,0},{9,11},{1... | collective-permute-start | bytes 958472 | tf_op jit(solution)/shard_map/ppermute | solution.py:56
  32.6 9.6 %collective-permute-start.6 = (bf16[32,4608]{1,0:T(8,128)(2,1)}, bf16[32,4608]{1,0:T(8,128)(2,1)}, u32[]{:S(2)}, u32[]{:S(2)}) collective-permute-start(bf16[32,4608]{1,0:T(8,128)(2,1)} %constant_dynamic-update-slice_fusion.refs_0_), channel_id=1, source_target_pairs={{0,4},{1,9},{2,6},{3,11},{4,0},{5,13},{6,2},{7,15},{8,12},{9,1},{1... | collective-permute-start | bytes 884744 | tf_op jit(solution)/shard_map/ppermute | solution.py:56
  35.3 8.3 %collective-permute-start.17 = (bf16[32,4992]{1,0:T(8,128)(2,1)S(1)}, bf16[32,4992]{1,0:T(8,128)(2,1)}, u32[]{:S(2)}, u32[]{:S(2)}) collective-permute-start(bf16[32,4992]{1,0:T(8,128)(2,1)S(1)} %collective-permute-done.16.refs_2_.refs_9_), channel_id=1, source_target_pairs={{0,8},{1,3},{2,10},{3,1},{4,12},{5,7},{6,14},{7,5},{8,0},{9,11},{1... | collective-permute-start | bytes 958472 | tf_op jit(solution)/shard_map/ppermute | solution.py:56
  37.4 9.8 %collective-permute-start.20 = (bf16[32,4992]{1,0:T(8,128)(2,1)S(1)}, bf16[32,4992]{1,0:T(8,128)(2,1)S(1)}, u32[]{:S(2)}, u32[]{:S(2)}) collective-permute-start(bf16[32,4992]{1,0:T(8,128)(2,1)S(1)} %collective-permute-done.16.refs_2_.refs_9_), channel_id=1, source_target_pairs={{0,1},{1,0},{2,3},{3,2},{4,5},{5,4},{6,7},{7,6},{8,9},{9,8},{10,11... | collective-permute-start | bytes 958472 | tf_op jit(solution)/shard_map/ppermute | solution.py:60
  38.4 10.0 %collective-permute-start.15 = (bf16[32,4992]{1,0:T(8,128)(2,1)S(1)}, bf16[32,4992]{1,0:T(8,128)(2,1)S(1)}, u32[]{:S(2)}, u32[]{:S(2)}) collective-permute-start(bf16[32,4992]{1,0:T(8,128)(2,1)S(1)} %collective-permute-done.14.refs_0_.refs_10_), channel_id=1, source_target_pairs={{0,1},{1,0},{2,3},{3,2},{4,5},{5,4},{6,7},{7,6},{8,9},{9,8},{10,11... | collective-permute-start | bytes 958472 | tf_op jit(solution)/shard_map/ppermute | solution.py:60
  39.2 8.1 %collective-permute-start.9 = (bf16[32,4608]{1,0:T(8,128)(2,1)}, bf16[32,4608]{1,0:T(8,128)(2,1)}, u32[]{:S(2)}, u32[]{:S(2)}) collective-permute-start(bf16[32,4608]{1,0:T(8,128)(2,1)} %constant_dynamic-update-slice_fusion.refs_0_), channel_id=1, source_target_pairs={{0,2},{1,5},{2,0},{3,7},{4,6},{5,1},{6,4},{7,3},{8,10},{9,13},{10,... | collective-permute-start | bytes 884744 | tf_op jit(solution)/shard_map/ppermute | solution.py:56
  42.2 8.2 %collective-permute-start.7 = (bf16[32,4608]{1,0:T(8,128)(2,1)}, bf16[32,4608]{1,0:T(8,128)(2,1)}, u32[]{:S(2)}, u32[]{:S(2)}) collective-permute-start(bf16[32,4608]{1,0:T(8,128)(2,1)} %collective-permute-done.6.refs_2_), channel_id=1, source_target_pairs={{0,2},{1,5},{2,0},{3,7},{4,6},{5,1},{6,4},{7,3},{8,10},{9,13},{10,... | collective-permute-start | bytes 884744 | tf_op jit(solution)/shard_map/ppermute | solution.py:56
  43.6 15.2 %collective-permute-start.18 = (bf16[32,4992]{1,0:T(8,128)(2,1)}, bf16[32,4992]{1,0:T(8,128)(2,1)}, u32[]{:S(2)}, u32[]{:S(2)}) collective-permute-start(bf16[32,4992]{1,0:T(8,128)(2,1)} %collective-permute-done.17.refs_2_.refs_11_), channel_id=1, source_target_pairs={{0,1},{1,0},{2,3},{3,2},{4,5},{5,4},{6,7},{7,6},{8,9},{9,8},{10,11... | collective-permute-start | bytes 958472 | tf_op jit(solution)/shard_map/ppermute | solution.py:60
  47.2 15.5 %collective-permute-start.11 = (bf16[32,4608]{1,0:T(8,128)(2,1)}, bf16[32,4608]{1,0:T(8,128)(2,1)}, u32[]{:S(2)}, u32[]{:S(2)}) collective-permute-start(bf16[32,4608]{1,0:T(8,128)(2,1)} %constant_dynamic-update-slice_fusion.refs_0_), channel_id=1, source_target_pairs={{0,1},{1,0},{2,3},{3,2},{4,5},{5,4},{6,7},{7,6},{8,9},{9,8},{10,11... | collective-permute-start | bytes 884744 | tf_op jit(solution)/shard_map/ppermute | solution.py:60
  48.0 14.8 %collective-permute-start.12 = (bf16[32,4608]{1,0:T(8,128)(2,1)}, bf16[32,4608]{1,0:T(8,128)(2,1)}, u32[]{:S(2)}, u32[]{:S(2)}) collective-permute-start(bf16[32,4608]{1,0:T(8,128)(2,1)} %collective-permute-done.6.refs_2_), channel_id=1, source_target_pairs={{0,1},{1,0},{2,3},{3,2},{4,5},{5,4},{6,7},{7,6},{8,9},{9,8},{10,11... | collective-permute-start | bytes 884744 | tf_op jit(solution)/shard_map/ppermute | solution.py:60
  49.2 16.7 %collective-permute-start.10 = (bf16[32,4608]{1,0:T(8,128)(2,1)}, bf16[32,4608]{1,0:T(8,128)(2,1)}, u32[]{:S(2)}, u32[]{:S(2)}) collective-permute-start(bf16[32,4608]{1,0:T(8,128)(2,1)} %collective-permute-done.9.refs_0_), channel_id=1, source_target_pairs={{0,1},{1,0},{2,3},{3,2},{4,5},{5,4},{6,7},{7,6},{8,9},{9,8},{10,11... | collective-permute-start | bytes 884744 | tf_op jit(solution)/shard_map/ppermute | solution.py:60
  50.4 17.6 %collective-permute-start.8 = (bf16[32,4608]{1,0:T(8,128)(2,1)}, bf16[32,4608]{1,0:T(8,128)(2,1)}, u32[]{:S(2)}, u32[]{:S(2)}) collective-permute-start(bf16[32,4608]{1,0:T(8,128)(2,1)} %collective-permute-done.7.refs_0_), channel_id=1, source_target_pairs={{0,1},{1,0},{2,3},{3,2},{4,5},{5,4},{6,7},{7,6},{8,9},{9,8},{10,11... | collective-permute-start | bytes 884744 | tf_op jit(solution)/shard_map/ppermute | solution.py:60
  50.4 6.0 %copy-start.9 = (s32[2]{0:T(128)S(1)}, s32[2]{0:T(128)}, u32[]{:S(2)}) copy-start(s32[2]{0:T(128)} %len_ref.10) | copy-start | bytes 28
  (9 other events, 16.0 us)

commit v2 on v1

--- a/solution.py
+++ b/solution.py
@@ -125,19 +125,20 @@
     return lax.dot_general(a, b, (((1,), (1,)), ((), ())), preferred_element_type=f32)
 
 
-def decode(lens, pool, qe):
+def decode(lens, pool, qe, begin, end, before=None):
     rows, heads, _ = qe.shape
     pages, page_width = pool.shape
     per_row = pages // rows
     pairs = page_width // PAIR
 
-    def body(len_ref, pool_ref, q_ref, out_ref):
+    def body(len_ref, pool_ref, q_ref, *refs):
+        out_ref = refs[-1]
         key_rows = pairs * per_row
         s = iota((heads, key_rows), 1)
         pos = (s % per_row) * (2 * pairs) + 2 * (s // per_row)
         zero = jnp.zeros((heads, ROTARY_WIDTH), bf16)
-        done = []
-        for g in range(rows):
+        done = [] if before is None else [refs[0][...]]
+        for g in range(begin, end):
             even, odd, rope = stack_keys(pool_ref, slice(g * per_row, (g + 1) * per_row), page_width)
             nope_q = q_ref[g, :, 0:512]
             rope_q = q_ref[g, :, 512:576]
@@ -154,13 +155,21 @@
             out = jnp.dot(pe.astype(bf16), even, preferred_element_type=f32)
             out += jnp.dot(po.astype(bf16), odd, preferred_element_type=f32)
             done.append((out / den).astype(bf16))
+        done = jnp.concatenate(done, axis=0)
+        if before is None:
+            out_ref[...] = done
+            return
         i, j = iota((rows * heads, rows * heads), 0), iota((rows * heads, rows * heads), 1)
         swap = jnp.where(j == (i % rows) * heads + i // rows, 1.0, 0.0).astype(bf16)
-        done = jnp.dot(swap, jnp.concatenate(done, axis=0), preferred_element_type=f32)
+        done = jnp.dot(swap, done, preferred_element_type=f32)
         for h in range(heads):
             out_ref[:, h * LATENT_WIDTH : (h + 1) * LATENT_WIDTH] = done[h * rows : (h + 1) * rows, :].astype(bf16)
 
-    return call(body, 1, 2, [jax.ShapeDtypeStruct((rows, heads * LATENT_WIDTH), bf16)])(lens, pool, qe)
+    if before is None:
+        out = jax.ShapeDtypeStruct(((end - begin) * heads, LATENT_WIDTH), bf16)
+        return call(body, 1, 2, [out])(lens, pool, qe)
+    out = jax.ShapeDtypeStruct((rows, heads * LATENT_WIDTH), bf16)
+    return call(body, 1, 3, [out])(lens, pool, qe, before)
 
 
 def gather_pages(table, pool, suffix, streams, cap):
@@ -428,7 +437,9 @@
         sent += gather_pages(table, pool, suffix, streams, cap)
     qe, qo = prepare(prefill_queries[0], heads)
     dq = decode_queries.reshape(decode_queries.shape[0], -1, WIDTH)
-    decode_part = decode(decode_len, pool, dq)
+    middle = dq.shape[0] // 2
+    some = decode(decode_len, pool, dq, 0, middle)
+    decode_part = decode(decode_len, pool, dq, middle, dq.shape[0], some)
 
     orders = [((1, 2, 4), (2, 4, 1)), ((4, 2, 1), (1, 4, 2))]
     orders = [orders[n % 2] for n in range(len(streams))]
@@ -460,16 +471,19 @@
         came.append((own, other))
 
     row_block = 128
-    plan = []
+    pieces = []
     for n in range(len(streams)):
         own, other = came[n]
-        piece = [[(own[k], masks_of[n], k), (other[k], masks_of[n], 4 + k)] for k in range(4)]
-        plan.append((f"att{n}a", piece[0] + piece[1]))
-        if n < len(streams) - 1:
-            plan.append((f"att{n}b", piece[2] + piece[3]))
-        else:
-            plan.append((f"att{n}b", piece[2]))
-            plan.append((f"att{n}c", piece[3]))
+        pieces.append([[(own[k], masks_of[n], k), (other[k], masks_of[n], 4 + k)] for k in range(4)])
+    plan = [("att0a", pieces[0][0] + pieces[0][1])]
+    if len(streams) > 1:
+        plan += [("att1a", pieces[1][0]), ("att0b", pieces[0][2] + pieces[0][3])]
+        for n in range(1, len(streams)):
+            if n > 1:
+                plan.append((f"att{n}a", pieces[n][0]))
+            plan += [(f"att{n}b", pieces[n][1] + pieces[n][2]), (f"att{n}c", pieces[n][3])]
+    else:
+        plan += [("att0b", pieces[0][2]), ("att0c", pieces[0][3])]
     tail = "att0b" if len(streams) > 1 else plan[-1][0]
     state = None
     for n, (name, group) in enumerate(plan):

time: 72 us -> 68.6 us (0.953); the launches traced: 71 us -> 68.4 us
  local copies, waits for them, and re-layouts: 7.61 us -> 4.47 us
    reshape x1, local copies, waits for them, and re-layouts: 1.77 us -> 0.19 us  [program(): dq = decode_queries.reshape(decode_queries.shape[0], -1, WIDTH)]
    unnamed x25 -> x29, local copies, waits for them, and re-layouts: 5.07 us -> 4.17 us
    pallas_call x1 -> x2, Pallas kernels: 2.81 us -> 3.46 us  [the longest x1 2.17 us: decode(): return call(body, 1, 3, [out])(lens, pool, qe, before)]
  transfers between devices with their start and end apart: 21 -> 21, of which waited for: 10 -> 10; matrix products, arithmetic and copies ran while one was open for 5% -> 1% of each run, Pallas kernels for 22% -> 23%
where the time goes in v2:
time: 68.6 us; the launch traced here: 68.4 us
  starting transfers between devices  28.1 us (41%)
  Pallas kernels  19.4 us (28%)
  waiting for transfers between devices  14.6 us (21%)
  local copies, waits for them, and re-layouts  4.47 us (7%)
  between operations  0.9 us (1%)
  other arithmetic  0.82 us (1%)
    ppermute x13, starting transfers between devices, xperm(): return lax.ppermute(value, ('dp', 'tp'), pairs)  26.9 us
    ppermute x13, waiting for transfers between devices, xperm(): return lax.ppermute(value, ('dp', 'tp'), pairs)  14.6 us
    pallas_call x5, Pallas kernels, attend(): call(body, 1, n_in, outs, mib, scratch_shapes=scratch)  14.2 us
    unnamed x29, local copies, waits for them, and re-layouts  4.17 us
    pallas_call x1, Pallas kernels, decode(): return call(body, 1, 3, [out])(lens, pool, qe, before)  2.17 us
  transfers between devices with their start and end apart: 21, of which 10 were waited for; matrix products, arithmetic and copies ran while one was open for 1% of the time, Pallas kernels for 23%

profile of v2, /device:TPU:0, one launch (start us, length us, event | category | flops | bytes accessed | tf_op | source)
XLA Modules:
  0.0 68.4 jit_solution(3462145135501119706)
XLA Ops:
  1.5 3.0 %collective-permute-start = (s32[16,128]{1,0:T(8,128)S(1)}, s32[16,128]{1,0:T(8,128)S(1)}, u32[]{:S(2)}, u32[]{:S(2)}) collective-permute-start(s32[16,128]{1,0:T(8,128)S(1)} %shard_map.96), channel_id=1, source_target_pairs={{0,2},{1,3},{2,0},{3,1},{4,6},{5,7},{6,4},{7,5},{8,10},{9,11},{10,... | collective-permute-start | bytes 24584 | tf_op jit(solution)/shard_map/ppermute | solution.py:56
  4.5 1.6 %collective-permute-done = s32[16,128]{1,0:T(8,128)S(1)} collective-permute-done((s32[16,128]{1,0:T(8,128)S(1)}, s32[16,128]{1,0:T(8,128)S(1)}, u32[]{:S(2)}, u32[]{:S(2)}) %collective-permute-start) | collective-permute-done | bytes 8224 | tf_op jit(solution)/shard_map/ppermute | solution.py:56
  6.2 2.0 %collective-permute-start.1 = (s32[16,128]{1,0:T(8,128)S(1)}, s32[16,128]{1,0:T(8,128)S(1)}, u32[]{:S(2)}, u32[]{:S(2)}) collective-permute-start(s32[16,128]{1,0:T(8,128)S(1)} %add.14), channel_id=1, source_target_pairs={{0,4},{1,5},{2,6},{3,7},{4,0},{5,1},{6,2},{7,3},{8,12},{9,13},{10,... | collective-permute-start | bytes 24584 | tf_op jit(solution)/shard_map/ppermute | solution.py:56
  8.2 1.6 %collective-permute-done.1 = s32[16,128]{1,0:T(8,128)S(1)} collective-permute-done((s32[16,128]{1,0:T(8,128)S(1)}, s32[16,128]{1,0:T(8,128)S(1)}, u32[]{:S(2)}, u32[]{:S(2)}) %collective-permute-start.1) | collective-permute-done | bytes 8224 | tf_op jit(solution)/shard_map/ppermute | solution.py:56
  9.9 2.1 %collective-permute-start.2 = (s32[16,128]{1,0:T(8,128)S(1)}, s32[16,128]{1,0:T(8,128)S(1)}, u32[]{:S(2)}, u32[]{:S(2)}) collective-permute-start(s32[16,128]{1,0:T(8,128)S(1)} %add.15), channel_id=1, source_target_pairs={{0,8},{1,9},{2,10},{3,11},{4,12},{5,13},{6,14},{7,15},{8,0},{9,1},... | collective-permute-start | bytes 24584 | tf_op jit(solution)/shard_map/ppermute | solution.py:56
  11.9 1.6 %collective-permute-done.2 = s32[16,128]{1,0:T(8,128)S(1)} collective-permute-done((s32[16,128]{1,0:T(8,128)S(1)}, s32[16,128]{1,0:T(8,128)S(1)}, u32[]{:S(2)}, u32[]{:S(2)}) %collective-permute-start.2) | collective-permute-done | bytes 8224 | tf_op jit(solution)/shard_map/ppermute | solution.py:56
  13.6 3.0 %collective-permute-start.3 = (s32[16,128]{1,0:T(8,128)S(1)}, s32[16,128]{1,0:T(8,128)S(1)}, u32[]{:S(2)}, u32[]{:S(2)}) collective-permute-start(s32[16,128]{1,0:T(8,128)S(1)} %add.16.table_ref), channel_id=1, source_target_pairs={{0,16},{1,17},{2,18},{3,19},{4,20},{5,21},{6,22},{7,23},{8,24},{9,... | collective-permute-start | bytes 24584 | tf_op jit(solution)/shard_map/ppermute | solution.py:56
  18.7 3.1 %collective-permute-start.4 = (bf16[16,4608]{1,0:T(8,128)(2,1)S(1)}, bf16[16,4608]{1,0:T(8,128)(2,1)S(1)}, u32[]{:S(2)}, u32[]{:S(2)}) collective-permute-start(bf16[16,4608]{1,0:T(8,128)(2,1)S(1)} %shard_map.98), channel_id=1, source_target_pairs={{0,16},{1,17},{2,18},{3,19},{4,20},{5,21},{6,22},{7,23},{8,24},{9,... | collective-permute-start | bytes 442376 | tf_op jit(solution)/shard_map/ppermute | solution.py:56
  22.5 1.6 %collective-permute-start.12 = (bf16[16,4992]{1,0:T(8,128)(2,1)S(1)}, bf16[16,4992]{1,0:T(8,128)(2,1)S(1)}, u32[]{:S(2)}, u32[]{:S(2)}) collective-permute-start(bf16[16,4992]{1,0:T(8,128)(2,1)S(1)} %shard_map.100), channel_id=1, source_target_pairs={{0,2},{1,5},{2,0},{3,7},{4,6},{5,1},{6,4},{7,3},{8,10},{9,13},{10,... | collective-permute-start | bytes 479240 | tf_op jit(solution)/shard_map/ppermute | solution.py:56
  24.1 1.4 %collective-permute-done.4 = bf16[16,4608]{1,0:T(8,128)(2,1)S(1)} collective-permute-done((bf16[16,4608]{1,0:T(8,128)(2,1)S(1)}, bf16[16,4608]{1,0:T(8,128)(2,1)S(1)}, u32[]{:S(2)}, u32[]{:S(2)}) %collective-permute-start.4) | collective-permute-done | bytes 147488 | tf_op jit(solution)/shard_map/ppermute | solution.py:56
  25.5 2.4 %collective-permute-start.5 = (bf16[16,4608]{1,0:T(8,128)(2,1)S(1)}, bf16[16,4608]{1,0:T(8,128)(2,1)S(1)}, u32[]{:S(2)}, u32[]{:S(2)}) collective-permute-start(bf16[16,4608]{1,0:T(8,128)(2,1)S(1)} %collective-permute-done.4), channel_id=1, source_target_pairs={{0,8},{1,3},{2,10},{3,1},{4,12},{5,7},{6,14},{7,5},{8,0},{9,11},{1... | collective-permute-start | bytes 442376 | tf_op jit(solution)/shard_map/ppermute | solution.py:56
  27.9 1.6 %collective-permute-start.15 = (bf16[32,4992]{1,0:T(8,128)(2,1)S(1)}, bf16[32,4992]{1,0:T(8,128)(2,1)S(1)}, u32[]{:S(2)}, u32[]{:S(2)}) collective-permute-start(bf16[32,4992]{1,0:T(8,128)(2,1)S(1)} %pad_maximum_fusion.refs_0_.refs_8_), channel_id=1, source_target_pairs={{0,4},{1,9},{2,6},{3,11},{4,0},{5,13},{6,2},{7,15},{8,12},{9,1},{1... | collective-permute-start | bytes 958472 | tf_op jit(solution)/shard_map/ppermute | solution.py:56
  29.5 2.5 %collective-permute-start.13 = (bf16[32,4992]{1,0:T(8,128)(2,1)S(1)}, bf16[32,4992]{1,0:T(8,128)(2,1)}, u32[]{:S(2)}, u32[]{:S(2)}) collective-permute-start(bf16[32,4992]{1,0:T(8,128)(2,1)S(1)} %pad_maximum_fusion.refs_0_.refs_8_), channel_id=1, source_target_pairs={{0,8},{1,3},{2,10},{3,1},{4,12},{5,7},{6,14},{7,5},{8,0},{9,11},{1... | collective-permute-start | bytes 958472 | tf_op jit(solution)/shard_map/ppermute | solution.py:56
  32.6 2.4 %collective-permute-done.15.refs_2_.refs_9_ = bf16[32,4992]{1,0:T(8,128)(2,1)S(1)} collective-permute-done((bf16[32,4992]{1,0:T(8,128)(2,1)S(1)}, bf16[32,4992]{1,0:T(8,128)(2,1)S(1)}, u32[]{:S(2)}, u32[]{:S(2)}) %collective-permute-start.15) | collective-permute-done | bytes 319520 | tf_op jit(solution)/shard_map/ppermute | solution.py:56
  34.9 2.5 %collective-permute-start.16 = (bf16[32,4992]{1,0:T(8,128)(2,1)S(1)}, bf16[32,4992]{1,0:T(8,128)(2,1)}, u32[]{:S(2)}, u32[]{:S(2)}) collective-permute-start(bf16[32,4992]{1,0:T(8,128)(2,1)S(1)} %collective-permute-done.15.refs_2_.refs_9_), channel_id=1, source_target_pairs={{0,8},{1,3},{2,10},{3,1},{4,12},{5,7},{6,14},{7,5},{8,0},{9,11},{1... | collective-permute-start | bytes 958472 | tf_op jit(solution)/shard_map/ppermute | solution.py:56
  39.4 2.5 %collective-permute-start.10 = (bf16[32,4608]{1,0:T(8,128)(2,1)S(1)}, bf16[32,4608]{1,0:T(8,128)(2,1)}, u32[]{:S(2)}, u32[]{:S(2)}) collective-permute-start(bf16[32,4608]{1,0:T(8,128)(2,1)S(1)} %constant_dynamic-update-slice_fusion.refs_0_), channel_id=1, source_target_pairs={{0,2},{1,5},{2,0},{3,7},{4,6},{5,1},{6,4},{7,3},{8,10},{9,13},{10,... | collective-permute-start | bytes 884744 | tf_op jit(solution)/shard_map/ppermute | solution.py:56
  43.8 2.9 %collective-permute-done.10.refs_2_ = bf16[32,4608]{1,0:T(8,128)(2,1)} collective-permute-done((bf16[32,4608]{1,0:T(8,128)(2,1)S(1)}, bf16[32,4608]{1,0:T(8,128)(2,1)}, u32[]{:S(2)}, u32[]{:S(2)}) %collective-permute-start.10) | collective-permute-done | bytes 294944 | tf_op jit(solution)/shard_map/ppermute | solution.py:56
  47.9 1.9 %collective-permute-done.7.refs_0_ = bf16[32,4608]{1,0:T(8,128)(2,1)} collective-permute-done((bf16[32,4608]{1,0:T(8,128)(2,1)}, bf16[32,4608]{1,0:T(8,128)(2,1)}, u32[]{:S(2)}, u32[]{:S(2)}) %collective-permute-start.7) | collective-permute-done | bytes 294944 | tf_op jit(solution)/shard_map/ppermute | solution.py:56
  51.6 2.2 %shard_map.107 = bf16[4,16384]{1,0:T(4,128)(2,1)} custom-call(s32[4]{0:T(128)S(1)} %copy-done.11, bf16[128,4608]{1,0:T(8,128)(2,1)S(1)} %shard_map.97.pool_ref, bf16[4,32,576]{2,1,0:T(8,128)(2,1)S(1)} %reshape.11.q_ref, bf16[64,512]{1,0:T(8,128)(2,1)S(1)} %shard_map.106.refs_0_), custom_call_target="tpu_custom_call" | custom-call | tf_op jit(solution)/shard_map/pallas_call | solution.py:172
  54.1 2.4 %shard_map.101 = (f32[512,128]{1,0:T(8,128)S(1)}, f32[512,128]{1,0:T(8,128)S(1)}, f32[512,512]{1,0:T(8,128)S(1)}) custom-call(s32[2]{0:T(128)S(1)} %copy-done.10, bf16[512,640]{1,0:T(8,128)(2,1)S(1)} %get-tuple-element.18.qe_ref, bf16[512,640]{1,0:T(8,128)(2,1)S(1)} %get-tuple-element.19.qo_ref, bf16[32,4992]{1,0:T(8,128)(2,1)S(1)} %pad_maximum_fusion.refs_0_.refs_8_, ...), custom_call_target="tpu_custom_call" | custom-call | tf_op jit(solution)/shard_map/pallas_call | solution.py:404
  56.5 1.6 %shard_map.102 = (f32[512,128]{1,0:T(8,128)S(1)}, f32[512,128]{1,0:T(8,128)S(1)}, f32[512,512]{1,0:T(8,128)S(1)}) custom-call(s32[2]{0:T(128)S(1)} %copy-done.10, bf16[512,640]{1,0:T(8,128)(2,1)S(1)} %get-tuple-element.18.qe_ref, bf16[512,640]{1,0:T(8,128)(2,1)S(1)} %get-tuple-element.19.qo_ref, bf16[32,4608]{1,0:T(8,128)(2,1)S(1)} %copy-done.6, ...), custom_call_target="tpu_custom_call" | custom-call | tf_op jit(solution)/shard_map/pallas_call | solution.py:404
  58.1 4.1 %shard_map.103 = (f32[512,128]{1,0:T(8,128)S(1)}, f32[512,128]{1,0:T(8,128)S(1)}, f32[512,512]{1,0:T(8,128)S(1)}) custom-call(s32[2]{0:T(128)S(1)} %copy-done.10, bf16[512,640]{1,0:T(8,128)(2,1)S(1)} %get-tuple-element.18.qe_ref, bf16[512,640]{1,0:T(8,128)(2,1)S(1)} %get-tuple-element.19.qo_ref, bf16[32,4992]{1,0:T(8,128)(2,1)} %collective-permute-done.13.refs_0_.refs_10_, ...), custom_call_target="tpu_custom_call" | custom-call | tf_op jit(solution)/shard_map/pallas_call | solution.py:404
  62.2 3.2 %shard_map.104 = (f32[512,128]{1,0:T(8,128)S(1)}, f32[512,128]{1,0:T(8,128)S(1)}, f32[512,512]{1,0:T(8,128)S(1)}) custom-call(s32[2]{0:T(128)S(1)} %copy-done.10, bf16[512,640]{1,0:T(8,128)(2,1)S(1)} %get-tuple-element.18.qe_ref, bf16[512,640]{1,0:T(8,128)(2,1)S(1)} %get-tuple-element.19.qo_ref, bf16[32,4608]{1,0:T(8,128)(2,1)} %collective-permute-done.6.refs_0_, ...), custom_call_target="tpu_custom_call" | custom-call | tf_op jit(solution)/shard_map/pallas_call | solution.py:404
  65.4 3.0 %shard_map.105 = bf16[128,2048]{1,0:T(8,128)(2,1)} custom-call(s32[2]{0:T(128)S(1)} %copy-done.10, bf16[512,640]{1,0:T(8,128)(2,1)S(1)} %get-tuple-element.18.qe_ref, bf16[512,640]{1,0:T(8,128)(2,1)S(1)} %get-tuple-element.19.qo_ref, bf16[32,4608]{1,0:T(8,128)(2,1)} %collective-permute-done.7.refs_0_, bf16[32,4608]{1,0:T(8,128)(2,1)} %collective-permute-done.8.refs_1_, ...), custom_call_target="tpu_custom_call" | custom-call | tf_op jit(solution)/shard_map/pallas_call | solution.py:404
  (71 shorter events, 11.3 us)
Async XLA Ops:
  1.5 4.7 %collective-permute-start = (s32[16,128]{1,0:T(8,128)S(1)}, s32[16,128]{1,0:T(8,128)S(1)}, u32[]{:S(2)}, u32[]{:S(2)}) collective-permute-start(s32[16,128]{1,0:T(8,128)S(1)} %shard_map.96), channel_id=1, source_target_pairs={{0,2},{1,3},{2,0},{3,1},{4,6},{5,7},{6,4},{7,5},{8,10},{9,11},{10,... | collective-permute-start | bytes 24584 | tf_op jit(solution)/shard_map/ppermute | solution.py:56
  6.2 3.7 %collective-permute-start.1 = (s32[16,128]{1,0:T(8,128)S(1)}, s32[16,128]{1,0:T(8,128)S(1)}, u32[]{:S(2)}, u32[]{:S(2)}) collective-permute-start(s32[16,128]{1,0:T(8,128)S(1)} %add.14), channel_id=1, source_target_pairs={{0,4},{1,5},{2,6},{3,7},{4,0},{5,1},{6,2},{7,3},{8,12},{9,13},{10,... | collective-permute-start | bytes 24584 | tf_op jit(solution)/shard_map/ppermute | solution.py:56
  9.9 3.7 %collective-permute-start.2 = (s32[16,128]{1,0:T(8,128)S(1)}, s32[16,128]{1,0:T(8,128)S(1)}, u32[]{:S(2)}, u32[]{:S(2)}) collective-permute-start(s32[16,128]{1,0:T(8,128)S(1)} %add.15), channel_id=1, source_target_pairs={{0,8},{1,9},{2,10},{3,11},{4,12},{5,13},{6,14},{7,15},{8,0},{9,1},... | collective-permute-start | bytes 24584 | tf_op jit(solution)/shard_map/ppermute | solution.py:56
  13.6 4.7 %collective-permute-start.3 = (s32[16,128]{1,0:T(8,128)S(1)}, s32[16,128]{1,0:T(8,128)S(1)}, u32[]{:S(2)}, u32[]{:S(2)}) collective-permute-start(s32[16,128]{1,0:T(8,128)S(1)} %add.16.table_ref), channel_id=1, source_target_pairs={{0,16},{1,17},{2,18},{3,19},{4,20},{5,21},{6,22},{7,23},{8,24},{9,... | collective-permute-start | bytes 24584 | tf_op jit(solution)/shard_map/ppermute | solution.py:56
  18.7 6.8 %collective-permute-start.4 = (bf16[16,4608]{1,0:T(8,128)(2,1)S(1)}, bf16[16,4608]{1,0:T(8,128)(2,1)S(1)}, u32[]{:S(2)}, u32[]{:S(2)}) collective-permute-start(bf16[16,4608]{1,0:T(8,128)(2,1)S(1)} %shard_map.98), channel_id=1, source_target_pairs={{0,16},{1,17},{2,18},{3,19},{4,20},{5,21},{6,22},{7,23},{8,24},{9,... | collective-permute-start | bytes 442376 | tf_op jit(solution)/shard_map/ppermute | solution.py:56
  22.0 27.8 %copy-start.7 = (bf16[1,128,2304]{2,1,0:T(8,128)(2,1)S(1)}, bf16[1,128,2304]{2,1,0:T(8,128)(2,1)}, u32[]{:S(2)}) copy-start(bf16[1,128,2304]{2,1,0:T(8,128)(2,1)} %param.12) | copy-start | bytes 1769476
  22.5 27.6 %copy-start.12 = (bf16[4,18432]{1,0:T(4,128)(2,1)S(1)}, bf16[4,18432]{1,0:T(4,128)(2,1)}, u32[]{:S(2)}) copy-start(bf16[4,18432]{1,0:T(4,128)(2,1)} %param.14) | copy-start | bytes 442372
  22.5 27.8 %copy-start.11 = (s32[4]{0:T(128)S(1)}, s32[4]{0:T(128)}, u32[]{:S(2)}) copy-start(s32[4]{0:T(128)} %len_ref.13) | copy-start | bytes 52
  22.5 5.3 %collective-permute-start.12 = (bf16[16,4992]{1,0:T(8,128)(2,1)S(1)}, bf16[16,4992]{1,0:T(8,128)(2,1)S(1)}, u32[]{:S(2)}, u32[]{:S(2)}) collective-permute-start(bf16[16,4992]{1,0:T(8,128)(2,1)S(1)} %shard_map.100), channel_id=1, source_target_pairs={{0,2},{1,5},{2,0},{3,7},{4,6},{5,1},{6,4},{7,3},{8,10},{9,13},{10,... | collective-permute-start | bytes 479240 | tf_op jit(solution)/shard_map/ppermute | solution.py:56
  25.5 6.5 %collective-permute-start.5 = (bf16[16,4608]{1,0:T(8,128)(2,1)S(1)}, bf16[16,4608]{1,0:T(8,128)(2,1)S(1)}, u32[]{:S(2)}, u32[]{:S(2)}) collective-permute-start(bf16[16,4608]{1,0:T(8,128)(2,1)S(1)} %collective-permute-done.4), channel_id=1, source_target_pairs={{0,8},{1,3},{2,10},{3,1},{4,12},{5,7},{6,14},{7,5},{8,0},{9,11},{1... | collective-permute-start | bytes 442376 | tf_op jit(solution)/shard_map/ppermute | solution.py:56
  27.9 7.1 %collective-permute-start.15 = (bf16[32,4992]{1,0:T(8,128)(2,1)S(1)}, bf16[32,4992]{1,0:T(8,128)(2,1)S(1)}, u32[]{:S(2)}, u32[]{:S(2)}) collective-permute-start(bf16[32,4992]{1,0:T(8,128)(2,1)S(1)} %pad_maximum_fusion.refs_0_.refs_8_), channel_id=1, source_target_pairs={{0,4},{1,9},{2,6},{3,11},{4,0},{5,13},{6,2},{7,15},{8,12},{9,1},{1... | collective-permute-start | bytes 958472 | tf_op jit(solution)/shard_map/ppermute | solution.py:56
  29.5 8.0 %collective-permute-start.18 = (bf16[32,4992]{1,0:T(8,128)(2,1)S(1)}, bf16[32,4992]{1,0:T(8,128)(2,1)S(1)}, u32[]{:S(2)}, u32[]{:S(2)}) collective-permute-start(bf16[32,4992]{1,0:T(8,128)(2,1)S(1)} %pad_maximum_fusion.refs_0_.refs_8_), channel_id=1, source_target_pairs={{0,1},{1,0},{2,3},{3,2},{4,5},{5,4},{6,7},{7,6},{8,9},{9,8},{10,11... | collective-permute-start | bytes 958472 | tf_op jit(solution)/shard_map/ppermute | solution.py:60
  29.5 9.9 %collective-permute-start.13 = (bf16[32,4992]{1,0:T(8,128)(2,1)S(1)}, bf16[32,4992]{1,0:T(8,128)(2,1)}, u32[]{:S(2)}, u32[]{:S(2)}) collective-permute-start(bf16[32,4992]{1,0:T(8,128)(2,1)S(1)} %pad_maximum_fusion.refs_0_.refs_8_), channel_id=1, source_target_pairs={{0,8},{1,3},{2,10},{3,1},{4,12},{5,7},{6,14},{7,5},{8,0},{9,11},{1... | collective-permute-start | bytes 958472 | tf_op jit(solution)/shard_map/ppermute | solution.py:56
  32.0 10.6 %collective-permute-start.6 = (bf16[32,4608]{1,0:T(8,128)(2,1)S(1)}, bf16[32,4608]{1,0:T(8,128)(2,1)}, u32[]{:S(2)}, u32[]{:S(2)}) collective-permute-start(bf16[32,4608]{1,0:T(8,128)(2,1)S(1)} %constant_dynamic-update-slice_fusion.refs_0_), channel_id=1, source_target_pairs={{0,4},{1,9},{2,6},{3,11},{4,0},{5,13},{6,2},{7,15},{8,12},{9,1},{1... | collective-permute-start | bytes 884744 | tf_op jit(solution)/shard_map/ppermute | solution.py:56
  34.9 8.7 %collective-permute-start.16 = (bf16[32,4992]{1,0:T(8,128)(2,1)S(1)}, bf16[32,4992]{1,0:T(8,128)(2,1)}, u32[]{:S(2)}, u32[]{:S(2)}) collective-permute-start(bf16[32,4992]{1,0:T(8,128)(2,1)S(1)} %collective-permute-done.15.refs_2_.refs_9_), channel_id=1, source_target_pairs={{0,8},{1,3},{2,10},{3,1},{4,12},{5,7},{6,14},{7,5},{8,0},{9,11},{1... | collective-permute-start | bytes 958472 | tf_op jit(solution)/shard_map/ppermute | solution.py:56
  37.4 5.1 %collective-permute-start.20 = (bf16[32,4608]{1,0:T(8,128)(2,1)S(1)}, bf16[32,4608]{1,0:T(8,128)(2,1)S(1)}, u32[]{:S(2)}, u32[]{:S(2)}) collective-permute-start(bf16[32,4608]{1,0:T(8,128)(2,1)S(1)} %constant_dynamic-update-slice_fusion.refs_0_), channel_id=1, source_target_pairs={{0,1},{1,0},{2,3},{3,2},{4,5},{5,4},{6,7},{7,6},{8,9},{9,8},{10,11... | collective-permute-start | bytes 884744 | tf_op jit(solution)/shard_map/ppermute | solution.py:60
  38.2 8.5 %collective-permute-start.19 = (bf16[32,4992]{1,0:T(8,128)(2,1)S(1)}, bf16[32,4992]{1,0:T(8,128)(2,1)S(1)}, u32[]{:S(2)}, u32[]{:S(2)}) collective-permute-start(bf16[32,4992]{1,0:T(8,128)(2,1)S(1)} %collective-permute-done.15.refs_2_.refs_9_), channel_id=1, source_target_pairs={{0,1},{1,0},{2,3},{3,2},{4,5},{5,4},{6,7},{7,6},{8,9},{9,8},{10,11... | collective-permute-start | bytes 958472 | tf_op jit(solution)/shard_map/ppermute | solution.py:60
  39.4 7.3 %collective-permute-start.10 = (bf16[32,4608]{1,0:T(8,128)(2,1)S(1)}, bf16[32,4608]{1,0:T(8,128)(2,1)}, u32[]{:S(2)}, u32[]{:S(2)}) collective-permute-start(bf16[32,4608]{1,0:T(8,128)(2,1)S(1)} %constant_dynamic-update-slice_fusion.refs_0_), channel_id=1, source_target_pairs={{0,2},{1,5},{2,0},{3,7},{4,6},{5,1},{6,4},{7,3},{8,10},{9,13},{10,... | collective-permute-start | bytes 884744 | tf_op jit(solution)/shard_map/ppermute | solution.py:56
  42.6 7.3 %collective-permute-start.7 = (bf16[32,4608]{1,0:T(8,128)(2,1)}, bf16[32,4608]{1,0:T(8,128)(2,1)}, u32[]{:S(2)}, u32[]{:S(2)}) collective-permute-start(bf16[32,4608]{1,0:T(8,128)(2,1)} %collective-permute-done.6.refs_0_), channel_id=1, source_target_pairs={{0,2},{1,5},{2,0},{3,7},{4,6},{5,1},{6,4},{7,3},{8,10},{9,13},{10,... | collective-permute-start | bytes 884744 | tf_op jit(solution)/shard_map/ppermute | solution.py:56
  43.3 14.8 %collective-permute-start.14 = (bf16[32,4992]{1,0:T(8,128)(2,1)}, bf16[32,4992]{1,0:T(8,128)(2,1)}, u32[]{:S(2)}, u32[]{:S(2)}) collective-permute-start(bf16[32,4992]{1,0:T(8,128)(2,1)} %collective-permute-done.13.refs_0_.refs_10_), channel_id=1, source_target_pairs={{0,1},{1,0},{2,3},{3,2},{4,5},{5,4},{6,7},{7,6},{8,9},{9,8},{10,11... | collective-permute-start | bytes 958472 | tf_op jit(solution)/shard_map/ppermute | solution.py:60
  43.6 14.5 %collective-permute-start.17 = (bf16[32,4992]{1,0:T(8,128)(2,1)}, bf16[32,4992]{1,0:T(8,128)(2,1)}, u32[]{:S(2)}, u32[]{:S(2)}) collective-permute-start(bf16[32,4992]{1,0:T(8,128)(2,1)} %collective-permute-done.16.refs_2_.refs_11_), channel_id=1, source_target_pairs={{0,1},{1,0},{2,3},{3,2},{4,5},{5,4},{6,7},{7,6},{8,9},{9,8},{10,11... | collective-permute-start | bytes 958472 | tf_op jit(solution)/shard_map/ppermute | solution.py:60
  46.7 15.5 %collective-permute-start.9 = (bf16[32,4608]{1,0:T(8,128)(2,1)}, bf16[32,4608]{1,0:T(8,128)(2,1)}, u32[]{:S(2)}, u32[]{:S(2)}) collective-permute-start(bf16[32,4608]{1,0:T(8,128)(2,1)} %collective-permute-done.6.refs_0_), channel_id=1, source_target_pairs={{0,1},{1,0},{2,3},{3,2},{4,5},{5,4},{6,7},{7,6},{8,9},{9,8},{10,11... | collective-permute-start | bytes 884744 | tf_op jit(solution)/shard_map/ppermute | solution.py:60
  47.4 14.8 %collective-permute-start.11 = (bf16[32,4608]{1,0:T(8,128)(2,1)}, bf16[32,4608]{1,0:T(8,128)(2,1)}, u32[]{:S(2)}, u32[]{:S(2)}) collective-permute-start(bf16[32,4608]{1,0:T(8,128)(2,1)} %collective-permute-done.10.refs_2_), channel_id=1, source_target_pairs={{0,1},{1,0},{2,3},{3,2},{4,5},{5,4},{6,7},{7,6},{8,9},{9,8},{10,11... | collective-permute-start | bytes 884744 | tf_op jit(solution)/shard_map/ppermute | solution.py:60
  49.8 15.6 %collective-permute-start.8 = (bf16[32,4608]{1,0:T(8,128)(2,1)}, bf16[32,4608]{1,0:T(8,128)(2,1)}, u32[]{:S(2)}, u32[]{:S(2)}) collective-permute-start(bf16[32,4608]{1,0:T(8,128)(2,1)} %collective-permute-done.7.refs_0_), channel_id=1, source_target_pairs={{0,1},{1,0},{2,3},{3,2},{4,5},{5,4},{6,7},{7,6},{8,9},{9,8},{10,11... | collective-permute-start | bytes 884744 | tf_op jit(solution)/shard_map/ppermute | solution.py:60
  (11 other events, 24.0 us)

commit v3 on v2

--- a/solution.py
+++ b/solution.py
@@ -50,9 +50,9 @@
     )
 
 
-def xperm(value, masks):
+def xperm(value, masks, flip=0):
     n, cores = lax.axis_size("dp"), lax.axis_size("tp")
-    pairs = [(d * cores + c, (d ^ masks[c % 2]) * cores + c) for d in range(n) for c in range(cores)]
+    pairs = [(d * cores + c, (d ^ masks[c]) * cores + (c ^ flip)) for d in range(n) for c in range(cores)]
     return lax.ppermute(value, ("dp", "tp"), pairs)
 
 
@@ -192,7 +192,7 @@
             at = 0
             for first, half in streams:
                 inside = (n >= at) & (n < at + half)
-                g = jnp.where(inside, n - at + core * half, g)
+                g = jnp.where(inside, n - at + (core if first == 0 else 1 - core) * half, g)
                 base = jnp.where(inside, first, base)
                 at += half
             return base, g
@@ -237,9 +237,9 @@
         for n, (base, half) in enumerate(streams):
             total = TEAM * half
             for side in range(2):
-                owner = (core + side) % 2
                 p = iota((width, total), 1)
                 b, i = p // half, p % half
+                owner = (core + side + b // 4) % 2
                 away = jnp.zeros((width, total), jnp.int32)
                 for k in range(3):
                     step = jnp.where(owner == 0, orders[n][0][k], orders[n][1][k])
@@ -248,7 +248,7 @@
                 holder = (team ^ (base + g // block)) * TEAM + (member ^ away)
                 sel = jnp.where(iota((width, total), 0) == holder * cap + g % cap, 1.0, 0.0).astype(bf16)
                 q = iota((ranks, total), 1)
-                asker = team * TEAM + ((owner * half + q % half) % block) // cap
+                asker = team * TEAM + (((core + side + q // (4 * half)) % 2 * half + q % half) % block) // cap
                 found = jnp.dot(tab, sel, preferred_element_type=f32)
                 found = jnp.sum(jnp.where(iota((ranks, total), 0) == asker, found, 0.0), axis=0, keepdims=True)
                 found = jnp.where(found > 0.0, 0.0, masked_score)
@@ -308,7 +308,7 @@
         rows = slice((b % 2) * half, (b % 2) * half + share)
         mine, theirs = came[b // 2][rows, page_width:], came[4 + b // 2][rows, page_width:]
         for side in range(2):
-            piece = jnp.where(core == side, mine, theirs)
+            piece = jnp.where(core == side ^ (b // 4), mine, theirs)
             source = member ^ sum(orders[side][k] for k in range(3) if (b >> k) & 1)
             at = pl.ds(pl.multiple_of(source * share, share), share)
             if side == 0:
@@ -427,7 +427,7 @@
     sent = []
     step = 1
     while step < ranks:
-        table = table + xperm(table, (step, step))
+        table = table + xperm(table, (step, step), 1)
         step *= 2
         if step == TEAM and split:
             sent += gather_pages(table, pool, suffix, streams[:1], cap)
@@ -441,7 +441,7 @@
     some = decode(decode_len, pool, dq, 0, middle)
     decode_part = decode(decode_len, pool, dq, middle, dq.shape[0], some)
 
-    orders = [((1, 2, 4), (2, 4, 1)), ((4, 2, 1), (1, 4, 2))]
+    orders = [((4, 1, 2), (4, 2, 1)), ((1, 2, 4), (2, 4, 1))]
     orders = [orders[n % 2] for n in range(len(streams))]
     masks_of = key_masks(table, streams, cap, orders, page_width // WIDTH)
 
@@ -453,7 +453,7 @@
         for at in range(0, half, unit):
             masks = tuple(TEAM * (base + (c * half + at) // block) for c in range(2))
             piece = rows[at : at + unit, :page_width] if half > unit else rows
-            pieces.append(xperm(piece, masks) if any(masks) else piece)
+            pieces.append(xperm(piece, masks, int(split)) if any(masks) else piece)
         if half > unit:
             rows = jnp.concatenate([jnp.concatenate(pieces, axis=0), rows[:, page_width:]], axis=1)
         else:
@@ -462,8 +462,8 @@
         got = xperm(rows, masks[0])
         both = jnp.concatenate([rows, got], axis=0)
         second = xperm(both, masks[1])
-        third = xperm(both, masks[2])
-        fourth = xperm(second, masks[2])
+        third = xperm(both, masks[2], 1)
+        fourth = xperm(second, masks[2], 1)
         own = [both, second, third, fourth]
         other = []
         for piece in own:

time: 68.6 us -> 69.9 us (1.019)
  waiting for transfers between devices: 14.6 us -> 18.4 us
  starting transfers between devices: 28.1 us -> 25.4 us
    ppermute x13, starting transfers between devices: 26.9 us -> 21.2 us  [xperm(): return lax.ppermute(value, ('dp', 'tp'), pairs)]
    ppermute x13, waiting for transfers between devices: 14.6 us -> 18.4 us  [xperm(): return lax.ppermute(value, ('dp', 'tp'), pairs)]
    ppermute x8, starting transfers between devices: 1.19 us -> 4.16 us  [sibling(): return lax.ppermute(value, 'tp', [(0, 1), (1, 0)])]
  transfers between devices with their start and end apart: 21 -> 21, of which waited for: 10 -> 9; matrix products, arithmetic and copies ran while one was open for 1% -> 1% of each run, Pallas kernels for 23% -> 23%
where the time goes in v3:
time: 69.9 us; the launch traced here: 69.5 us
  starting transfers between devices  25.4 us (36%)
  Pallas kernels  19.4 us (28%)
  waiting for transfers between devices  18.4 us (26%)
  local copies, waits for them, and re-layouts  4.47 us (6%)
  between operations  0.91 us (1%)
  other arithmetic  0.82 us (1%)
    ppermute x13, starting transfers between devices, xperm(): return lax.ppermute(value, ('dp', 'tp'), pairs)  21.2 us
    ppermute x13, waiting for transfers between devices, xperm(): return lax.ppermute(value, ('dp', 'tp'), pairs)  18.4 us
    pallas_call x5, Pallas kernels, attend(): call(body, 1, n_in, outs, mib, scratch_shapes=scratch)  14.2 us
    unnamed x29, local copies, waits for them, and re-layouts  4.17 us
    ppermute x8, starting transfers between devices, sibling(): return lax.ppermute(value, 'tp', [(0, 1), (1, 0)])  4.16 us
    pallas_call x1, Pallas kernels, decode(): return call(body, 1, 3, [out])(lens, pool, qe, before)  2.17 us
  transfers between devices with their start and end apart: 21, of which 9 were waited for; matrix products, arithmetic and copies ran while one was open for 1% of the time, Pallas kernels for 23%

profile of v3, /device:TPU:0, one launch (start us, length us, event | category | flops | bytes accessed | tf_op | source)
XLA Modules:
  0.0 69.5 jit_solution(1559404658004797403)
XLA Ops:
  1.5 2.5 %collective-permute-start = (s32[16,128]{1,0:T(8,128)S(1)}, s32[16,128]{1,0:T(8,128)S(1)}, u32[]{:S(2)}, u32[]{:S(2)}) collective-permute-start(s32[16,128]{1,0:T(8,128)S(1)} %shard_map.96), channel_id=1, source_target_pairs={{0,3},{1,2},{2,1},{3,0},{4,7},{5,6},{6,5},{7,4},{8,11},{9,10},{10,... | collective-permute-start | bytes 24584 | tf_op jit(solution)/shard_map/ppermute | solution.py:56
  4.0 1.4 %collective-permute-done = s32[16,128]{1,0:T(8,128)S(1)} collective-permute-done((s32[16,128]{1,0:T(8,128)S(1)}, s32[16,128]{1,0:T(8,128)S(1)}, u32[]{:S(2)}, u32[]{:S(2)}) %collective-permute-start) | collective-permute-done | bytes 8224 | tf_op jit(solution)/shard_map/ppermute | solution.py:56
  5.4 2.1 %collective-permute-start.1 = (s32[16,128]{1,0:T(8,128)S(1)}, s32[16,128]{1,0:T(8,128)S(1)}, u32[]{:S(2)}, u32[]{:S(2)}) collective-permute-start(s32[16,128]{1,0:T(8,128)S(1)} %add.14), channel_id=1, source_target_pairs={{0,5},{1,4},{2,7},{3,6},{4,1},{5,0},{6,3},{7,2},{8,13},{9,12},{10,... | collective-permute-start | bytes 24584 | tf_op jit(solution)/shard_map/ppermute | solution.py:56
  7.4 1.4 %collective-permute-done.1 = s32[16,128]{1,0:T(8,128)S(1)} collective-permute-done((s32[16,128]{1,0:T(8,128)S(1)}, s32[16,128]{1,0:T(8,128)S(1)}, u32[]{:S(2)}, u32[]{:S(2)}) %collective-permute-start.1) | collective-permute-done | bytes 8224 | tf_op jit(solution)/shard_map/ppermute | solution.py:56
  8.8 1.8 %collective-permute-start.2 = (s32[16,128]{1,0:T(8,128)S(1)}, s32[16,128]{1,0:T(8,128)S(1)}, u32[]{:S(2)}, u32[]{:S(2)}) collective-permute-start(s32[16,128]{1,0:T(8,128)S(1)} %add.15), channel_id=1, source_target_pairs={{0,9},{1,8},{2,11},{3,10},{4,13},{5,12},{6,15},{7,14},{8,1},{9,0},... | collective-permute-start | bytes 24584 | tf_op jit(solution)/shard_map/ppermute | solution.py:56
  10.5 1.4 %collective-permute-done.2 = s32[16,128]{1,0:T(8,128)S(1)} collective-permute-done((s32[16,128]{1,0:T(8,128)S(1)}, s32[16,128]{1,0:T(8,128)S(1)}, u32[]{:S(2)}, u32[]{:S(2)}) %collective-permute-start.2) | collective-permute-done | bytes 8224 | tf_op jit(solution)/shard_map/ppermute | solution.py:56
  11.9 2.7 %collective-permute-start.3 = (s32[16,128]{1,0:T(8,128)S(1)}, s32[16,128]{1,0:T(8,128)S(1)}, u32[]{:S(2)}, u32[]{:S(2)}) collective-permute-start(s32[16,128]{1,0:T(8,128)S(1)} %add.16.table_ref), channel_id=1, source_target_pairs={{0,17},{1,16},{2,19},{3,18},{4,21},{5,20},{6,23},{7,22},{8,25},{9,... | collective-permute-start | bytes 24584 | tf_op jit(solution)/shard_map/ppermute | solution.py:56
  16.6 2.5 %collective-permute-start.4 = (bf16[16,4608]{1,0:T(8,128)(2,1)S(1)}, bf16[16,4608]{1,0:T(8,128)(2,1)S(1)}, u32[]{:S(2)}, u32[]{:S(2)}) collective-permute-start(bf16[16,4608]{1,0:T(8,128)(2,1)S(1)} %shard_map.98), channel_id=1, source_target_pairs={{0,17},{1,16},{2,19},{3,18},{4,21},{5,20},{6,23},{7,22},{8,25},{9,... | collective-permute-start | bytes 442376 | tf_op jit(solution)/shard_map/ppermute | solution.py:56
  19.8 1.6 %collective-permute-start.12 = (bf16[16,4992]{1,0:T(8,128)(2,1)S(1)}, bf16[16,4992]{1,0:T(8,128)(2,1)S(1)}, u32[]{:S(2)}, u32[]{:S(2)}) collective-permute-start(bf16[16,4992]{1,0:T(8,128)(2,1)S(1)} %shard_map.100), channel_id=1, source_target_pairs={{0,8},{1,9},{2,10},{3,11},{4,12},{5,13},{6,14},{7,15},{8,0},{9,1},... | collective-permute-start | bytes 479240 | tf_op jit(solution)/shard_map/ppermute | solution.py:56
  21.5 5.0 %collective-permute-done.4 = bf16[16,4608]{1,0:T(8,128)(2,1)S(1)} collective-permute-done((bf16[16,4608]{1,0:T(8,128)(2,1)S(1)}, bf16[16,4608]{1,0:T(8,128)(2,1)S(1)}, u32[]{:S(2)}, u32[]{:S(2)}) %collective-permute-start.4) | collective-permute-done | bytes 147488 | tf_op jit(solution)/shard_map/ppermute | solution.py:56
  26.4 1.8 %collective-permute-start.5 = (bf16[16,4608]{1,0:T(8,128)(2,1)S(1)}, bf16[16,4608]{1,0:T(8,128)(2,1)S(1)}, u32[]{:S(2)}, u32[]{:S(2)}) collective-permute-start(bf16[16,4608]{1,0:T(8,128)(2,1)S(1)} %collective-permute-done.4), channel_id=1, source_target_pairs={{0,2},{1,5},{2,0},{3,7},{4,6},{5,1},{6,4},{7,3},{8,10},{9,13},{10,... | collective-permute-start | bytes 442376 | tf_op jit(solution)/shard_map/ppermute | solution.py:56
  28.3 1.7 %collective-permute-start.15 = (bf16[32,4992]{1,0:T(8,128)(2,1)S(1)}, bf16[32,4992]{1,0:T(8,128)(2,1)S(1)}, u32[]{:S(2)}, u32[]{:S(2)}) collective-permute-start(bf16[32,4992]{1,0:T(8,128)(2,1)S(1)} %pad_maximum_fusion.refs_0_.refs_8_), channel_id=1, source_target_pairs={{0,2},{1,5},{2,0},{3,7},{4,6},{5,1},{6,4},{7,3},{8,10},{9,13},{10,... | collective-permute-start | bytes 958472 | tf_op jit(solution)/shard_map/ppermute | solution.py:56
  30.0 1.6 %collective-permute-start.13 = (bf16[32,4992]{1,0:T(8,128)(2,1)S(1)}, bf16[32,4992]{1,0:T(8,128)(2,1)}, u32[]{:S(2)}, u32[]{:S(2)}) collective-permute-start(bf16[32,4992]{1,0:T(8,128)(2,1)S(1)} %pad_maximum_fusion.refs_0_.refs_8_), channel_id=1, source_target_pairs={{0,5},{1,2},{2,7},{3,0},{4,1},{5,6},{6,3},{7,4},{8,13},{9,10},{10,... | collective-permute-start | bytes 958472 | tf_op jit(solution)/shard_map/ppermute | solution.py:56
  31.7 1.8 %collective-permute-start.6 = (bf16[32,4608]{1,0:T(8,128)(2,1)S(1)}, bf16[32,4608]{1,0:T(8,128)(2,1)}, u32[]{:S(2)}, u32[]{:S(2)}) collective-permute-start(bf16[32,4608]{1,0:T(8,128)(2,1)S(1)} %constant_dynamic-update-slice_fusion.refs_0_), channel_id=1, source_target_pairs={{0,4},{1,9},{2,6},{3,11},{4,0},{5,13},{6,2},{7,15},{8,12},{9,1},{1... | collective-permute-start | bytes 884744 | tf_op jit(solution)/shard_map/ppermute | solution.py:56
  33.5 4.3 %collective-permute-done.15.refs_2_.refs_9_ = bf16[32,4992]{1,0:T(8,128)(2,1)S(1)} collective-permute-done((bf16[32,4992]{1,0:T(8,128)(2,1)S(1)}, bf16[32,4992]{1,0:T(8,128)(2,1)S(1)}, u32[]{:S(2)}, u32[]{:S(2)}) %collective-permute-start.15) | collective-permute-done | bytes 319520 | tf_op jit(solution)/shard_map/ppermute | solution.py:56
  37.8 2.5 %collective-permute-start.20 = (bf16[32,4608]{1,0:T(8,128)(2,1)S(1)}, bf16[32,4608]{1,0:T(8,128)(2,1)S(1)}, u32[]{:S(2)}, u32[]{:S(2)}) collective-permute-start(bf16[32,4608]{1,0:T(8,128)(2,1)S(1)} %constant_dynamic-update-slice_fusion.refs_0_), channel_id=1, source_target_pairs={{0,1},{1,0},{2,3},{3,2},{4,5},{5,4},{6,7},{7,6},{8,9},{9,8},{10,11... | collective-permute-start | bytes 884744 | tf_op jit(solution)/shard_map/ppermute | solution.py:60
  44.7 2.7 %collective-permute-done.10.refs_2_ = bf16[32,4608]{1,0:T(8,128)(2,1)} collective-permute-done((bf16[32,4608]{1,0:T(8,128)(2,1)S(1)}, bf16[32,4608]{1,0:T(8,128)(2,1)}, u32[]{:S(2)}, u32[]{:S(2)}) %collective-permute-start.10) | collective-permute-done | bytes 294944 | tf_op jit(solution)/shard_map/ppermute | solution.py:56
  48.8 1.8 %collective-permute-done.7.refs_0_ = bf16[32,4608]{1,0:T(8,128)(2,1)} collective-permute-done((bf16[32,4608]{1,0:T(8,128)(2,1)}, bf16[32,4608]{1,0:T(8,128)(2,1)}, u32[]{:S(2)}, u32[]{:S(2)}) %collective-permute-start.7) | collective-permute-done | bytes 294944 | tf_op jit(solution)/shard_map/ppermute | solution.py:56
  52.7 2.2 %shard_map.107 = bf16[4,16384]{1,0:T(4,128)(2,1)} custom-call(s32[4]{0:T(128)S(1)} %copy-done.11, bf16[128,4608]{1,0:T(8,128)(2,1)S(1)} %shard_map.97.pool_ref, bf16[4,32,576]{2,1,0:T(8,128)(2,1)S(1)} %reshape.11.q_ref, bf16[64,512]{1,0:T(8,128)(2,1)S(1)} %shard_map.106.refs_0_), custom_call_target="tpu_custom_call" | custom-call | tf_op jit(solution)/shard_map/pallas_call | solution.py:172
  55.2 2.4 %shard_map.101 = (f32[512,128]{1,0:T(8,128)S(1)}, f32[512,128]{1,0:T(8,128)S(1)}, f32[512,512]{1,0:T(8,128)S(1)}) custom-call(s32[2]{0:T(128)S(1)} %copy-done.10, bf16[512,640]{1,0:T(8,128)(2,1)S(1)} %get-tuple-element.18.qe_ref, bf16[512,640]{1,0:T(8,128)(2,1)S(1)} %get-tuple-element.19.qo_ref, bf16[32,4992]{1,0:T(8,128)(2,1)S(1)} %pad_maximum_fusion.refs_0_.refs_8_, ...), custom_call_target="tpu_custom_call" | custom-call | tf_op jit(solution)/shard_map/pallas_call | solution.py:404
  57.6 1.6 %shard_map.102 = (f32[512,128]{1,0:T(8,128)S(1)}, f32[512,128]{1,0:T(8,128)S(1)}, f32[512,512]{1,0:T(8,128)S(1)}) custom-call(s32[2]{0:T(128)S(1)} %copy-done.10, bf16[512,640]{1,0:T(8,128)(2,1)S(1)} %get-tuple-element.18.qe_ref, bf16[512,640]{1,0:T(8,128)(2,1)S(1)} %get-tuple-element.19.qo_ref, bf16[32,4608]{1,0:T(8,128)(2,1)S(1)} %copy-done.6, ...), custom_call_target="tpu_custom_call" | custom-call | tf_op jit(solution)/shard_map/pallas_call | solution.py:404
  59.2 4.1 %shard_map.103 = (f32[512,128]{1,0:T(8,128)S(1)}, f32[512,128]{1,0:T(8,128)S(1)}, f32[512,512]{1,0:T(8,128)S(1)}) custom-call(s32[2]{0:T(128)S(1)} %copy-done.10, bf16[512,640]{1,0:T(8,128)(2,1)S(1)} %get-tuple-element.18.qe_ref, bf16[512,640]{1,0:T(8,128)(2,1)S(1)} %get-tuple-element.19.qo_ref, bf16[32,4992]{1,0:T(8,128)(2,1)} %collective-permute-done.13.refs_0_.refs_10_, ...), custom_call_target="tpu_custom_call" | custom-call | tf_op jit(solution)/shard_map/pallas_call | solution.py:404
  63.3 3.1 %shard_map.104 = (f32[512,128]{1,0:T(8,128)S(1)}, f32[512,128]{1,0:T(8,128)S(1)}, f32[512,512]{1,0:T(8,128)S(1)}) custom-call(s32[2]{0:T(128)S(1)} %copy-done.10, bf16[512,640]{1,0:T(8,128)(2,1)S(1)} %get-tuple-element.18.qe_ref, bf16[512,640]{1,0:T(8,128)(2,1)S(1)} %get-tuple-element.19.qo_ref, bf16[32,4608]{1,0:T(8,128)(2,1)} %collective-permute-done.6.refs_0_, ...), custom_call_target="tpu_custom_call" | custom-call | tf_op jit(solution)/shard_map/pallas_call | solution.py:404
  66.5 3.0 %shard_map.105 = bf16[128,2048]{1,0:T(8,128)(2,1)} custom-call(s32[2]{0:T(128)S(1)} %copy-done.10, bf16[512,640]{1,0:T(8,128)(2,1)S(1)} %get-tuple-element.18.qe_ref, bf16[512,640]{1,0:T(8,128)(2,1)S(1)} %get-tuple-element.19.qo_ref, bf16[32,4608]{1,0:T(8,128)(2,1)} %collective-permute-done.7.refs_0_, bf16[32,4608]{1,0:T(8,128)(2,1)} %collective-permute-done.8.refs_1_, ...), custom_call_target="tpu_custom_call" | custom-call | tf_op jit(solution)/shard_map/pallas_call | solution.py:404
  (71 shorter events, 11.8 us)
Async XLA Ops:
  1.5 3.8 %collective-permute-start = (s32[16,128]{1,0:T(8,128)S(1)}, s32[16,128]{1,0:T(8,128)S(1)}, u32[]{:S(2)}, u32[]{:S(2)}) collective-permute-start(s32[16,128]{1,0:T(8,128)S(1)} %shard_map.96), channel_id=1, source_target_pairs={{0,3},{1,2},{2,1},{3,0},{4,7},{5,6},{6,5},{7,4},{8,11},{9,10},{10,... | collective-permute-start | bytes 24584 | tf_op jit(solution)/shard_map/ppermute | solution.py:56
  5.4 3.4 %collective-permute-start.1 = (s32[16,128]{1,0:T(8,128)S(1)}, s32[16,128]{1,0:T(8,128)S(1)}, u32[]{:S(2)}, u32[]{:S(2)}) collective-permute-start(s32[16,128]{1,0:T(8,128)S(1)} %add.14), channel_id=1, source_target_pairs={{0,5},{1,4},{2,7},{3,6},{4,1},{5,0},{6,3},{7,2},{8,13},{9,12},{10,... | collective-permute-start | bytes 24584 | tf_op jit(solution)/shard_map/ppermute | solution.py:56
  8.8 3.1 %collective-permute-start.2 = (s32[16,128]{1,0:T(8,128)S(1)}, s32[16,128]{1,0:T(8,128)S(1)}, u32[]{:S(2)}, u32[]{:S(2)}) collective-permute-start(s32[16,128]{1,0:T(8,128)S(1)} %add.15), channel_id=1, source_target_pairs={{0,9},{1,8},{2,11},{3,10},{4,13},{5,12},{6,15},{7,14},{8,1},{9,0},... | collective-permute-start | bytes 24584 | tf_op jit(solution)/shard_map/ppermute | solution.py:56
  11.9 4.2 %collective-permute-start.3 = (s32[16,128]{1,0:T(8,128)S(1)}, s32[16,128]{1,0:T(8,128)S(1)}, u32[]{:S(2)}, u32[]{:S(2)}) collective-permute-start(s32[16,128]{1,0:T(8,128)S(1)} %add.16.table_ref), channel_id=1, source_target_pairs={{0,17},{1,16},{2,19},{3,18},{4,21},{5,20},{6,23},{7,22},{8,25},{9,... | collective-permute-start | bytes 24584 | tf_op jit(solution)/shard_map/ppermute | solution.py:56
  16.6 9.8 %collective-permute-start.4 = (bf16[16,4608]{1,0:T(8,128)(2,1)S(1)}, bf16[16,4608]{1,0:T(8,128)(2,1)S(1)}, u32[]{:S(2)}, u32[]{:S(2)}) collective-permute-start(bf16[16,4608]{1,0:T(8,128)(2,1)S(1)} %shard_map.98), channel_id=1, source_target_pairs={{0,17},{1,16},{2,19},{3,18},{4,21},{5,20},{6,23},{7,22},{8,25},{9,... | collective-permute-start | bytes 442376 | tf_op jit(solution)/shard_map/ppermute | solution.py:56
  19.3 31.6 %copy-start.7 = (bf16[1,128,2304]{2,1,0:T(8,128)(2,1)S(1)}, bf16[1,128,2304]{2,1,0:T(8,128)(2,1)}, u32[]{:S(2)}) copy-start(bf16[1,128,2304]{2,1,0:T(8,128)(2,1)} %param.12) | copy-start | bytes 1769476
  19.8 31.3 %copy-start.12 = (bf16[4,18432]{1,0:T(4,128)(2,1)S(1)}, bf16[4,18432]{1,0:T(4,128)(2,1)}, u32[]{:S(2)}) copy-start(bf16[4,18432]{1,0:T(4,128)(2,1)} %param.14) | copy-start | bytes 442372
  19.8 31.5 %copy-start.11 = (s32[4]{0:T(128)S(1)}, s32[4]{0:T(128)}, u32[]{:S(2)}) copy-start(s32[4]{0:T(128)} %len_ref.13) | copy-start | bytes 52
  19.8 8.5 %collective-permute-start.12 = (bf16[16,4992]{1,0:T(8,128)(2,1)S(1)}, bf16[16,4992]{1,0:T(8,128)(2,1)S(1)}, u32[]{:S(2)}, u32[]{:S(2)}) collective-permute-start(bf16[16,4992]{1,0:T(8,128)(2,1)S(1)} %shard_map.100), channel_id=1, source_target_pairs={{0,8},{1,9},{2,10},{3,11},{4,12},{5,13},{6,14},{7,15},{8,0},{9,1},... | collective-permute-start | bytes 479240 | tf_op jit(solution)/shard_map/ppermute | solution.py:56
  26.4 5.2 %collective-permute-start.5 = (bf16[16,4608]{1,0:T(8,128)(2,1)S(1)}, bf16[16,4608]{1,0:T(8,128)(2,1)S(1)}, u32[]{:S(2)}, u32[]{:S(2)}) collective-permute-start(bf16[16,4608]{1,0:T(8,128)(2,1)S(1)} %collective-permute-done.4), channel_id=1, source_target_pairs={{0,2},{1,5},{2,0},{3,7},{4,6},{5,1},{6,4},{7,3},{8,10},{9,13},{10,... | collective-permute-start | bytes 442376 | tf_op jit(solution)/shard_map/ppermute | solution.py:56
  28.3 9.5 %collective-permute-start.15 = (bf16[32,4992]{1,0:T(8,128)(2,1)S(1)}, bf16[32,4992]{1,0:T(8,128)(2,1)S(1)}, u32[]{:S(2)}, u32[]{:S(2)}) collective-permute-start(bf16[32,4992]{1,0:T(8,128)(2,1)S(1)} %pad_maximum_fusion.refs_0_.refs_8_), channel_id=1, source_target_pairs={{0,2},{1,5},{2,0},{3,7},{4,6},{5,1},{6,4},{7,3},{8,10},{9,13},{10,... | collective-permute-start | bytes 958472 | tf_op jit(solution)/shard_map/ppermute | solution.py:56
  30.0 10.3 %collective-permute-start.18 = (bf16[32,4992]{1,0:T(8,128)(2,1)S(1)}, bf16[32,4992]{1,0:T(8,128)(2,1)S(1)}, u32[]{:S(2)}, u32[]{:S(2)}) collective-permute-start(bf16[32,4992]{1,0:T(8,128)(2,1)S(1)} %pad_maximum_fusion.refs_0_.refs_8_), channel_id=1, source_target_pairs={{0,1},{1,0},{2,3},{3,2},{4,5},{5,4},{6,7},{7,6},{8,9},{9,8},{10,11... | collective-permute-start | bytes 958472 | tf_op jit(solution)/shard_map/ppermute | solution.py:60
  30.0 11.0 %collective-permute-start.13 = (bf16[32,4992]{1,0:T(8,128)(2,1)S(1)}, bf16[32,4992]{1,0:T(8,128)(2,1)}, u32[]{:S(2)}, u32[]{:S(2)}) collective-permute-start(bf16[32,4992]{1,0:T(8,128)(2,1)S(1)} %pad_maximum_fusion.refs_0_.refs_8_), channel_id=1, source_target_pairs={{0,5},{1,2},{2,7},{3,0},{4,1},{5,6},{6,3},{7,4},{8,13},{9,10},{10,... | collective-permute-start | bytes 958472 | tf_op jit(solution)/shard_map/ppermute | solution.py:56
  31.7 11.2 %collective-permute-start.6 = (bf16[32,4608]{1,0:T(8,128)(2,1)S(1)}, bf16[32,4608]{1,0:T(8,128)(2,1)}, u32[]{:S(2)}, u32[]{:S(2)}) collective-permute-start(bf16[32,4608]{1,0:T(8,128)(2,1)S(1)} %constant_dynamic-update-slice_fusion.refs_0_), channel_id=1, source_target_pairs={{0,4},{1,9},{2,6},{3,11},{4,0},{5,13},{6,2},{7,15},{8,12},{9,1},{1... | collective-permute-start | bytes 884744 | tf_op jit(solution)/shard_map/ppermute | solution.py:56
  37.8 6.5 %collective-permute-start.16 = (bf16[32,4992]{1,0:T(8,128)(2,1)S(1)}, bf16[32,4992]{1,0:T(8,128)(2,1)}, u32[]{:S(2)}, u32[]{:S(2)}) collective-permute-start(bf16[32,4992]{1,0:T(8,128)(2,1)S(1)} %collective-permute-done.15.refs_2_.refs_9_), channel_id=1, source_target_pairs={{0,5},{1,2},{2,7},{3,0},{4,1},{5,6},{6,3},{7,4},{8,13},{9,10},{10,... | collective-permute-start | bytes 958472 | tf_op jit(solution)/shard_map/ppermute | solution.py:56
  37.8 5.1 %collective-permute-start.20 = (bf16[32,4608]{1,0:T(8,128)(2,1)S(1)}, bf16[32,4608]{1,0:T(8,128)(2,1)S(1)}, u32[]{:S(2)}, u32[]{:S(2)}) collective-permute-start(bf16[32,4608]{1,0:T(8,128)(2,1)S(1)} %constant_dynamic-update-slice_fusion.refs_0_), channel_id=1, source_target_pairs={{0,1},{1,0},{2,3},{3,2},{4,5},{5,4},{6,7},{7,6},{8,9},{9,8},{10,11... | collective-permute-start | bytes 884744 | tf_op jit(solution)/shard_map/ppermute | solution.py:60
  41.0 7.1 %collective-permute-start.19 = (bf16[32,4992]{1,0:T(8,128)(2,1)S(1)}, bf16[32,4992]{1,0:T(8,128)(2,1)S(1)}, u32[]{:S(2)}, u32[]{:S(2)}) collective-permute-start(bf16[32,4992]{1,0:T(8,128)(2,1)S(1)} %collective-permute-done.15.refs_2_.refs_9_), channel_id=1, source_target_pairs={{0,1},{1,0},{2,3},{3,2},{4,5},{5,4},{6,7},{7,6},{8,9},{9,8},{10,11... | collective-permute-start | bytes 958472 | tf_op jit(solution)/shard_map/ppermute | solution.py:60
  41.0 6.4 %collective-permute-start.10 = (bf16[32,4608]{1,0:T(8,128)(2,1)S(1)}, bf16[32,4608]{1,0:T(8,128)(2,1)}, u32[]{:S(2)}, u32[]{:S(2)}) collective-permute-start(bf16[32,4608]{1,0:T(8,128)(2,1)S(1)} %constant_dynamic-update-slice_fusion.refs_0_), channel_id=1, source_target_pairs={{0,9},{1,2},{2,11},{3,0},{4,13},{5,6},{6,15},{7,4},{8,1},{9,10},{1... | collective-permute-start | bytes 884744 | tf_op jit(solution)/shard_map/ppermute | solution.py:56
  42.8 7.7 %collective-permute-start.7 = (bf16[32,4608]{1,0:T(8,128)(2,1)}, bf16[32,4608]{1,0:T(8,128)(2,1)}, u32[]{:S(2)}, u32[]{:S(2)}) collective-permute-start(bf16[32,4608]{1,0:T(8,128)(2,1)} %collective-permute-done.6.refs_0_), channel_id=1, source_target_pairs={{0,9},{1,2},{2,11},{3,0},{4,13},{5,6},{6,15},{7,4},{8,1},{9,10},{1... | collective-permute-start | bytes 884744 | tf_op jit(solution)/shard_map/ppermute | solution.py:56
  43.6 15.6 %collective-permute-start.14 = (bf16[32,4992]{1,0:T(8,128)(2,1)}, bf16[32,4992]{1,0:T(8,128)(2,1)}, u32[]{:S(2)}, u32[]{:S(2)}) collective-permute-start(bf16[32,4992]{1,0:T(8,128)(2,1)} %collective-permute-done.13.refs_0_.refs_10_), channel_id=1, source_target_pairs={{0,1},{1,0},{2,3},{3,2},{4,5},{5,4},{6,7},{7,6},{8,9},{9,8},{10,11... | collective-permute-start | bytes 958472 | tf_op jit(solution)/shard_map/ppermute | solution.py:60
  44.3 14.9 %collective-permute-start.17 = (bf16[32,4992]{1,0:T(8,128)(2,1)}, bf16[32,4992]{1,0:T(8,128)(2,1)}, u32[]{:S(2)}, u32[]{:S(2)}) collective-permute-start(bf16[32,4992]{1,0:T(8,128)(2,1)} %collective-permute-done.16.refs_2_.refs_11_), channel_id=1, source_target_pairs={{0,1},{1,0},{2,3},{3,2},{4,5},{5,4},{6,7},{7,6},{8,9},{9,8},{10,11... | collective-permute-start | bytes 958472 | tf_op jit(solution)/shard_map/ppermute | solution.py:60
  47.4 15.9 %collective-permute-start.9 = (bf16[32,4608]{1,0:T(8,128)(2,1)}, bf16[32,4608]{1,0:T(8,128)(2,1)}, u32[]{:S(2)}, u32[]{:S(2)}) collective-permute-start(bf16[32,4608]{1,0:T(8,128)(2,1)} %collective-permute-done.6.refs_0_), channel_id=1, source_target_pairs={{0,1},{1,0},{2,3},{3,2},{4,5},{5,4},{6,7},{7,6},{8,9},{9,8},{10,11... | collective-permute-start | bytes 884744 | tf_op jit(solution)/shard_map/ppermute | solution.py:60
  48.8 14.5 %collective-permute-start.11 = (bf16[32,4608]{1,0:T(8,128)(2,1)}, bf16[32,4608]{1,0:T(8,128)(2,1)}, u32[]{:S(2)}, u32[]{:S(2)}) collective-permute-start(bf16[32,4608]{1,0:T(8,128)(2,1)} %collective-permute-done.10.refs_2_), channel_id=1, source_target_pairs={{0,1},{1,0},{2,3},{3,2},{4,5},{5,4},{6,7},{7,6},{8,9},{9,8},{10,11... | collective-permute-start | bytes 884744 | tf_op jit(solution)/shard_map/ppermute | solution.py:60
  50.6 15.9 %collective-permute-start.8 = (bf16[32,4608]{1,0:T(8,128)(2,1)}, bf16[32,4608]{1,0:T(8,128)(2,1)}, u32[]{:S(2)}, u32[]{:S(2)}) collective-permute-start(bf16[32,4608]{1,0:T(8,128)(2,1)} %collective-permute-done.7.refs_0_), channel_id=1, source_target_pairs={{0,1},{1,0},{2,3},{3,2},{4,5},{5,4},{6,7},{7,6},{8,9},{9,8},{10,11... | collective-permute-start | bytes 884744 | tf_op jit(solution)/shard_map/ppermute | solution.py:60
  (11 other events, 23.3 us)

commit v4 on v3

--- a/solution.py
+++ b/solution.py
@@ -475,15 +475,15 @@
     for n in range(len(streams)):
         own, other = came[n]
         pieces.append([[(own[k], masks_of[n], k), (other[k], masks_of[n], 4 + k)] for k in range(4)])
-    plan = [("att0a", pieces[0][0] + pieces[0][1])]
     if len(streams) > 1:
-        plan += [("att1a", pieces[1][0]), ("att0b", pieces[0][2] + pieces[0][3])]
+        plan = [("att0a", pieces[0][0]), ("att0f", pieces[0][1]), ("att1a", pieces[1][0])]
+        plan += [("att0e", pieces[0][2]), ("att0b", pieces[0][3])]
         for n in range(1, len(streams)):
             if n > 1:
                 plan.append((f"att{n}a", pieces[n][0]))
-            plan += [(f"att{n}b", pieces[n][1] + pieces[n][2]), (f"att{n}c", pieces[n][3])]
+            plan += [(f"att{n}b", pieces[n][1]), (f"att{n}d", pieces[n][2]), (f"att{n}c", pieces[n][3])]
     else:
-        plan += [("att0b", pieces[0][2]), ("att0c", pieces[0][3])]
+        plan = [("att0a", pieces[0][0] + pieces[0][1]), ("att0b", pieces[0][2]), ("att0c", pieces[0][3])]
     tail = "att0b" if len(streams) > 1 else plan[-1][0]
     state = None
     for n, (name, group) in enumerate(plan):

time: 69.9 us -> 73.3 us (1.049)
  Pallas kernels: 19.4 us -> 22.1 us
  waiting for transfers between devices: 18.4 us -> 19.5 us
  starting transfers between devices: 25.4 us -> 24.4 us
  local copies, waits for them, and re-layouts: 4.47 us -> 5.21 us
    pallas_call x5 -> x8, Pallas kernels: 14.2 us -> 16.8 us  [attend(): call(body, 1, n_in, outs, mib, scratch_shapes=scratch)]
    ppermute x13, waiting for transfers between devices: 18.4 us -> 19.5 us  [xperm(): return lax.ppermute(value, ('dp', 'tp'), pairs)]
    unnamed x29 -> x33, local copies, waits for them, and re-layouts: 4.17 us -> 4.9 us
  transfers between devices with their start and end apart: 21 -> 21, of which waited for: 9 -> 8; matrix products, arithmetic and copies ran while one was open for 1% -> 1% of each run, Pallas kernels for 23% -> 25%
where the time goes in v4:
time: 73.3 us; the launch traced here: 73 us
  starting transfers between devices  24.4 us (33%)
  Pallas kernels  22.1 us (30%)
  waiting for transfers between devices  19.5 us (27%)
  local copies, waits for them, and re-layouts  5.21 us (7%)
  between operations  0.94 us (1%)
  other arithmetic  0.83 us (1%)
    ppermute x13, starting transfers between devices, xperm(): return lax.ppermute(value, ('dp', 'tp'), pairs)  20.9 us
    ppermute x13, waiting for transfers between devices, xperm(): return lax.ppermute(value, ('dp', 'tp'), pairs)  19.5 us
    pallas_call x8, Pallas kernels, attend(): call(body, 1, n_in, outs, mib, scratch_shapes=scratch)  16.8 us
    unnamed x33, local copies, waits for them, and re-layouts  4.9 us
    ppermute x8, starting transfers between devices, sibling(): return lax.ppermute(value, 'tp', [(0, 1), (1, 0)])  3.53 us
    pallas_call x1, Pallas kernels, decode(): return call(body, 1, 3, [out])(lens, pool, qe, before)  2.16 us
  transfers between devices with their start and end apart: 21, of which 8 were waited for; matrix products, arithmetic and copies ran while one was open for 1% of the time, Pallas kernels for 25%

profile of v4, /device:TPU:0, one launch (start us, length us, event | category | flops | bytes accessed | tf_op | source)
XLA Modules:
  0.0 73.0 jit_solution(508998268137502926)
XLA Ops:
  1.5 2.5 %collective-permute-start = (s32[16,128]{1,0:T(8,128)S(1)}, s32[16,128]{1,0:T(8,128)S(1)}, u32[]{:S(2)}, u32[]{:S(2)}) collective-permute-start(s32[16,128]{1,0:T(8,128)S(1)} %shard_map.96), channel_id=1, source_target_pairs={{0,3},{1,2},{2,1},{3,0},{4,7},{5,6},{6,5},{7,4},{8,11},{9,10},{10,... | collective-permute-start | bytes 24584 | tf_op jit(solution)/shard_map/ppermute | solution.py:56
  5.4 2.1 %collective-permute-start.1 = (s32[16,128]{1,0:T(8,128)S(1)}, s32[16,128]{1,0:T(8,128)S(1)}, u32[]{:S(2)}, u32[]{:S(2)}) collective-permute-start(s32[16,128]{1,0:T(8,128)S(1)} %add.14), channel_id=1, source_target_pairs={{0,5},{1,4},{2,7},{3,6},{4,1},{5,0},{6,3},{7,2},{8,13},{9,12},{10,... | collective-permute-start | bytes 24584 | tf_op jit(solution)/shard_map/ppermute | solution.py:56
  8.8 1.8 %collective-permute-start.2 = (s32[16,128]{1,0:T(8,128)S(1)}, s32[16,128]{1,0:T(8,128)S(1)}, u32[]{:S(2)}, u32[]{:S(2)}) collective-permute-start(s32[16,128]{1,0:T(8,128)S(1)} %add.15), channel_id=1, source_target_pairs={{0,9},{1,8},{2,11},{3,10},{4,13},{5,12},{6,15},{7,14},{8,1},{9,0},... | collective-permute-start | bytes 24584 | tf_op jit(solution)/shard_map/ppermute | solution.py:56
  11.9 2.7 %collective-permute-start.3 = (s32[16,128]{1,0:T(8,128)S(1)}, s32[16,128]{1,0:T(8,128)S(1)}, u32[]{:S(2)}, u32[]{:S(2)}) collective-permute-start(s32[16,128]{1,0:T(8,128)S(1)} %add.16.table_ref), channel_id=1, source_target_pairs={{0,17},{1,16},{2,19},{3,18},{4,21},{5,20},{6,23},{7,22},{8,25},{9,... | collective-permute-start | bytes 24584 | tf_op jit(solution)/shard_map/ppermute | solution.py:56
  16.6 2.5 %collective-permute-start.4 = (bf16[16,4608]{1,0:T(8,128)(2,1)S(1)}, bf16[16,4608]{1,0:T(8,128)(2,1)S(1)}, u32[]{:S(2)}, u32[]{:S(2)}) collective-permute-start(bf16[16,4608]{1,0:T(8,128)(2,1)S(1)} %shard_map.98), channel_id=1, source_target_pairs={{0,17},{1,16},{2,19},{3,18},{4,21},{5,20},{6,23},{7,22},{8,25},{9,... | collective-permute-start | bytes 442376 | tf_op jit(solution)/shard_map/ppermute | solution.py:56
  19.8 1.6 %collective-permute-start.12 = (bf16[16,4992]{1,0:T(8,128)(2,1)S(1)}, bf16[16,4992]{1,0:T(8,128)(2,1)S(1)}, u32[]{:S(2)}, u32[]{:S(2)}) collective-permute-start(bf16[16,4992]{1,0:T(8,128)(2,1)S(1)} %shard_map.100), channel_id=1, source_target_pairs={{0,8},{1,9},{2,10},{3,11},{4,12},{5,13},{6,14},{7,15},{8,0},{9,1},... | collective-permute-start | bytes 479240 | tf_op jit(solution)/shard_map/ppermute | solution.py:56
  21.5 5.0 %collective-permute-done.4 = bf16[16,4608]{1,0:T(8,128)(2,1)S(1)} collective-permute-done((bf16[16,4608]{1,0:T(8,128)(2,1)S(1)}, bf16[16,4608]{1,0:T(8,128)(2,1)S(1)}, u32[]{:S(2)}, u32[]{:S(2)}) %collective-permute-start.4) | collective-permute-done | bytes 147488 | tf_op jit(solution)/shard_map/ppermute | solution.py:56
  26.4 1.8 %collective-permute-start.5 = (bf16[16,4608]{1,0:T(8,128)(2,1)S(1)}, bf16[16,4608]{1,0:T(8,128)(2,1)S(1)}, u32[]{:S(2)}, u32[]{:S(2)}) collective-permute-start(bf16[16,4608]{1,0:T(8,128)(2,1)S(1)} %collective-permute-done.4), channel_id=1, source_target_pairs={{0,2},{1,5},{2,0},{3,7},{4,6},{5,1},{6,4},{7,3},{8,10},{9,13},{10,... | collective-permute-start | bytes 442376 | tf_op jit(solution)/shard_map/ppermute | solution.py:56
  28.4 1.7 %collective-permute-start.13 = (bf16[32,4992]{1,0:T(8,128)(2,1)S(1)}, bf16[32,4992]{1,0:T(8,128)(2,1)S(1)}, u32[]{:S(2)}, u32[]{:S(2)}) collective-permute-start(bf16[32,4992]{1,0:T(8,128)(2,1)S(1)} %pad_maximum_fusion.refs_0_.refs_4_), channel_id=1, source_target_pairs={{0,2},{1,5},{2,0},{3,7},{4,6},{5,1},{6,4},{7,3},{8,10},{9,13},{10,... | collective-permute-start | bytes 958472 | tf_op jit(solution)/shard_map/ppermute | solution.py:56
  30.2 1.4 %collective-permute-done.5 = bf16[16,4608]{1,0:T(8,128)(2,1)S(1)} collective-permute-done((bf16[16,4608]{1,0:T(8,128)(2,1)S(1)}, bf16[16,4608]{1,0:T(8,128)(2,1)S(1)}, u32[]{:S(2)}, u32[]{:S(2)}) %collective-permute-start.5) | collective-permute-done | bytes 147488 | tf_op jit(solution)/shard_map/ppermute | solution.py:56
  31.7 1.8 %collective-permute-start.6 = (bf16[32,4608]{1,0:T(8,128)(2,1)S(1)}, bf16[32,4608]{1,0:T(8,128)(2,1)}, u32[]{:S(2)}, u32[]{:S(2)}) collective-permute-start(bf16[32,4608]{1,0:T(8,128)(2,1)S(1)} %constant_dynamic-update-slice_fusion.refs_0_), channel_id=1, source_target_pairs={{0,4},{1,9},{2,6},{3,11},{4,0},{5,13},{6,2},{7,15},{8,12},{9,1},{1... | collective-permute-start | bytes 884744 | tf_op jit(solution)/shard_map/ppermute | solution.py:56
  33.5 4.3 %collective-permute-done.13.refs_0_.refs_5_ = bf16[32,4992]{1,0:T(8,128)(2,1)S(1)} collective-permute-done((bf16[32,4992]{1,0:T(8,128)(2,1)S(1)}, bf16[32,4992]{1,0:T(8,128)(2,1)S(1)}, u32[]{:S(2)}, u32[]{:S(2)}) %collective-permute-start.13) | collective-permute-done | bytes 319520 | tf_op jit(solution)/shard_map/ppermute | solution.py:56
  39.0 1.4 %collective-permute-start.20 = (bf16[32,4608]{1,0:T(8,128)(2,1)S(1)}, bf16[32,4608]{1,0:T(8,128)(2,1)S(1)}, u32[]{:S(2)}, u32[]{:S(2)}) collective-permute-start(bf16[32,4608]{1,0:T(8,128)(2,1)S(1)} %constant_dynamic-update-slice_fusion.refs_0_), channel_id=1, source_target_pairs={{0,1},{1,0},{2,3},{3,2},{4,5},{5,4},{6,7},{7,6},{8,9},{9,8},{10,11... | collective-permute-start | bytes 884744 | tf_op jit(solution)/shard_map/ppermute | solution.py:60
  45.1 3.0 %collective-permute-done.9.refs_0_ = bf16[32,4608]{1,0:T(8,128)(2,1)} collective-permute-done((bf16[32,4608]{1,0:T(8,128)(2,1)S(1)}, bf16[32,4608]{1,0:T(8,128)(2,1)}, u32[]{:S(2)}, u32[]{:S(2)}) %collective-permute-start.9) | collective-permute-done | bytes 294944 | tf_op jit(solution)/shard_map/ppermute | solution.py:56
  49.7 1.6 %collective-permute-done.7.refs_0_ = bf16[32,4608]{1,0:T(8,128)(2,1)} collective-permute-done((bf16[32,4608]{1,0:T(8,128)(2,1)}, bf16[32,4608]{1,0:T(8,128)(2,1)}, u32[]{:S(2)}, u32[]{:S(2)}) %collective-permute-start.7) | collective-permute-done | bytes 294944 | tf_op jit(solution)/shard_map/ppermute | solution.py:56
  53.6 2.2 %shard_map.110 = bf16[4,16384]{1,0:T(4,128)(2,1)} custom-call(s32[4]{0:T(128)S(1)} %copy-done.13, bf16[128,4608]{1,0:T(8,128)(2,1)S(1)} %shard_map.97.pool_ref, bf16[4,32,576]{2,1,0:T(8,128)(2,1)S(1)} %reshape.11.q_ref, bf16[64,512]{1,0:T(8,128)(2,1)S(1)} %shard_map.109.refs_0_), custom_call_target="tpu_custom_call" | custom-call | tf_op jit(solution)/shard_map/pallas_call | solution.py:172
  56.0 1.5 %shard_map.101 = (f32[512,128]{1,0:T(8,128)S(1)}, f32[512,128]{1,0:T(8,128)S(1)}, f32[512,512]{1,0:T(8,128)S(1)}) custom-call(s32[2]{0:T(128)S(1)} %copy-done.12, bf16[512,640]{1,0:T(8,128)(2,1)S(1)} %get-tuple-element.27.qe_ref, bf16[512,640]{1,0:T(8,128)(2,1)S(1)} %get-tuple-element.28.qo_ref, bf16[32,4992]{1,0:T(8,128)(2,1)S(1)} %pad_maximum_fusion.refs_0_.refs_4_, ...), custom_call_target="tpu_custom_call" | custom-call | tf_op jit(solution)/shard_map/pallas_call | solution.py:404
  57.6 1.6 %shard_map.102 = (f32[512,128]{1,0:T(8,128)S(1)}, f32[512,128]{1,0:T(8,128)S(1)}, f32[512,512]{1,0:T(8,128)S(1)}) custom-call(s32[2]{0:T(128)S(1)} %copy-done.12, bf16[512,640]{1,0:T(8,128)(2,1)S(1)} %get-tuple-element.27.qe_ref, bf16[512,640]{1,0:T(8,128)(2,1)S(1)} %get-tuple-element.28.qo_ref, bf16[32,4992]{1,0:T(8,128)(2,1)S(1)} %copy-done.3, ...), custom_call_target="tpu_custom_call" | custom-call | tf_op jit(solution)/shard_map/pallas_call | solution.py:404
  59.2 1.6 %shard_map.103 = (f32[512,128]{1,0:T(8,128)S(1)}, f32[512,128]{1,0:T(8,128)S(1)}, f32[512,512]{1,0:T(8,128)S(1)}) custom-call(s32[2]{0:T(128)S(1)} %copy-done.12, bf16[512,640]{1,0:T(8,128)(2,1)S(1)} %get-tuple-element.27.qe_ref, bf16[512,640]{1,0:T(8,128)(2,1)S(1)} %get-tuple-element.28.qo_ref, bf16[32,4608]{1,0:T(8,128)(2,1)S(1)} %copy-done.8, ...), custom_call_target="tpu_custom_call" | custom-call | tf_op jit(solution)/shard_map/pallas_call | solution.py:404
  60.8 2.1 %shard_map.104 = (f32[512,128]{1,0:T(8,128)S(1)}, f32[512,128]{1,0:T(8,128)S(1)}, f32[512,512]{1,0:T(8,128)S(1)}) custom-call(s32[2]{0:T(128)S(1)} %copy-done.12, bf16[512,640]{1,0:T(8,128)(2,1)S(1)} %get-tuple-element.27.qe_ref, bf16[512,640]{1,0:T(8,128)(2,1)S(1)} %get-tuple-element.28.qo_ref, bf16[32,4992]{1,0:T(8,128)(2,1)} %collective-permute-done.16.refs_0_.refs_6_, ...), custom_call_target="tpu_custom_call" | custom-call | tf_op jit(solution)/shard_map/pallas_call | solution.py:404
  63.0 2.8 %shard_map.105 = (f32[512,128]{1,0:T(8,128)S(1)}, f32[512,128]{1,0:T(8,128)S(1)}, f32[512,512]{1,0:T(8,128)S(1)}) custom-call(s32[2]{0:T(128)S(1)} %copy-done.12, bf16[512,640]{1,0:T(8,128)(2,1)S(1)} %get-tuple-element.27.qe_ref, bf16[512,640]{1,0:T(8,128)(2,1)S(1)} %get-tuple-element.28.qo_ref, ...), custom_call_target="tpu_custom_call" | custom-call | tf_op jit(solution)/shard_map/pallas_call | solution.py:404
  65.8 2.1 %shard_map.106 = (f32[512,128]{1,0:T(8,128)S(1)}, f32[512,128]{1,0:T(8,128)S(1)}, f32[512,512]{1,0:T(8,128)S(1)}) custom-call(s32[2]{0:T(128)S(1)} %copy-done.12, bf16[512,640]{1,0:T(8,128)(2,1)S(1)} %get-tuple-element.27.qe_ref, bf16[512,640]{1,0:T(8,128)(2,1)S(1)} %get-tuple-element.28.qo_ref, bf16[32,4608]{1,0:T(8,128)(2,1)} %collective-permute-done.6.refs_0_, ...), custom_call_target="tpu_custom_call" | custom-call | tf_op jit(solution)/shard_map/pallas_call | solution.py:404
  67.9 2.1 %shard_map.107 = (f32[512,128]{1,0:T(8,128)S(1)}, f32[512,128]{1,0:T(8,128)S(1)}, f32[512,512]{1,0:T(8,128)S(1)}) custom-call(s32[2]{0:T(128)S(1)} %copy-done.12, bf16[512,640]{1,0:T(8,128)(2,1)S(1)} %get-tuple-element.27.qe_ref, bf16[512,640]{1,0:T(8,128)(2,1)S(1)} %get-tuple-element.28.qo_ref, bf16[32,4608]{1,0:T(8,128)(2,1)} %collective-permute-done.9.refs_0_, ...), custom_call_target="tpu_custom_call" | custom-call | tf_op jit(solution)/shard_map/pallas_call | solution.py:404
  70.1 2.9 %shard_map.108 = bf16[128,2048]{1,0:T(8,128)(2,1)} custom-call(s32[2]{0:T(128)S(1)} %copy-done.12, bf16[512,640]{1,0:T(8,128)(2,1)S(1)} %get-tuple-element.27.qe_ref, bf16[512,640]{1,0:T(8,128)(2,1)S(1)} %get-tuple-element.28.qo_ref, bf16[32,4608]{1,0:T(8,128)(2,1)} %collective-permute-done.7.refs_0_, bf16[32,4608]{1,0:T(8,128)(2,1)} %collective-permute-done.8.refs_1_, ...), custom_call_target="tpu_custom_call" | custom-call | tf_op jit(solution)/shard_map/pallas_call | solution.py:404
  (78 shorter events, 17.8 us)
Async XLA Ops:
  1.5 3.8 %collective-permute-start = (s32[16,128]{1,0:T(8,128)S(1)}, s32[16,128]{1,0:T(8,128)S(1)}, u32[]{:S(2)}, u32[]{:S(2)}) collective-permute-start(s32[16,128]{1,0:T(8,128)S(1)} %shard_map.96), channel_id=1, source_target_pairs={{0,3},{1,2},{2,1},{3,0},{4,7},{5,6},{6,5},{7,4},{8,11},{9,10},{10,... | collective-permute-start | bytes 24584 | tf_op jit(solution)/shard_map/ppermute | solution.py:56
  5.4 3.4 %collective-permute-start.1 = (s32[16,128]{1,0:T(8,128)S(1)}, s32[16,128]{1,0:T(8,128)S(1)}, u32[]{:S(2)}, u32[]{:S(2)}) collective-permute-start(s32[16,128]{1,0:T(8,128)S(1)} %add.14), channel_id=1, source_target_pairs={{0,5},{1,4},{2,7},{3,6},{4,1},{5,0},{6,3},{7,2},{8,13},{9,12},{10,... | collective-permute-start | bytes 24584 | tf_op jit(solution)/shard_map/ppermute | solution.py:56
  8.8 3.1 %collective-permute-start.2 = (s32[16,128]{1,0:T(8,128)S(1)}, s32[16,128]{1,0:T(8,128)S(1)}, u32[]{:S(2)}, u32[]{:S(2)}) collective-permute-start(s32[16,128]{1,0:T(8,128)S(1)} %add.15), channel_id=1, source_target_pairs={{0,9},{1,8},{2,11},{3,10},{4,13},{5,12},{6,15},{7,14},{8,1},{9,0},... | collective-permute-start | bytes 24584 | tf_op jit(solution)/shard_map/ppermute | solution.py:56
  11.9 4.2 %collective-permute-start.3 = (s32[16,128]{1,0:T(8,128)S(1)}, s32[16,128]{1,0:T(8,128)S(1)}, u32[]{:S(2)}, u32[]{:S(2)}) collective-permute-start(s32[16,128]{1,0:T(8,128)S(1)} %add.16.table_ref), channel_id=1, source_target_pairs={{0,17},{1,16},{2,19},{3,18},{4,21},{5,20},{6,23},{7,22},{8,25},{9,... | collective-permute-start | bytes 24584 | tf_op jit(solution)/shard_map/ppermute | solution.py:56
  16.6 9.8 %collective-permute-start.4 = (bf16[16,4608]{1,0:T(8,128)(2,1)S(1)}, bf16[16,4608]{1,0:T(8,128)(2,1)S(1)}, u32[]{:S(2)}, u32[]{:S(2)}) collective-permute-start(bf16[16,4608]{1,0:T(8,128)(2,1)S(1)} %shard_map.98), channel_id=1, source_target_pairs={{0,17},{1,16},{2,19},{3,18},{4,21},{5,20},{6,23},{7,22},{8,25},{9,... | collective-permute-start | bytes 442376 | tf_op jit(solution)/shard_map/ppermute | solution.py:56
  19.3 32.5 %copy-start.9 = (bf16[1,128,2304]{2,1,0:T(8,128)(2,1)S(1)}, bf16[1,128,2304]{2,1,0:T(8,128)(2,1)}, u32[]{:S(2)}) copy-start(bf16[1,128,2304]{2,1,0:T(8,128)(2,1)} %param.12) | copy-start | bytes 1769476
  19.8 32.2 %copy-start.14 = (bf16[4,18432]{1,0:T(4,128)(2,1)S(1)}, bf16[4,18432]{1,0:T(4,128)(2,1)}, u32[]{:S(2)}) copy-start(bf16[4,18432]{1,0:T(4,128)(2,1)} %param.14) | copy-start | bytes 442372
  19.8 32.4 %copy-start.13 = (s32[4]{0:T(128)S(1)}, s32[4]{0:T(128)}, u32[]{:S(2)}) copy-start(s32[4]{0:T(128)} %len_ref.19) | copy-start | bytes 52
  19.8 8.5 %collective-permute-start.12 = (bf16[16,4992]{1,0:T(8,128)(2,1)S(1)}, bf16[16,4992]{1,0:T(8,128)(2,1)S(1)}, u32[]{:S(2)}, u32[]{:S(2)}) collective-permute-start(bf16[16,4992]{1,0:T(8,128)(2,1)S(1)} %shard_map.100), channel_id=1, source_target_pairs={{0,8},{1,9},{2,10},{3,11},{4,12},{5,13},{6,14},{7,15},{8,0},{9,1},... | collective-permute-start | bytes 479240 | tf_op jit(solution)/shard_map/ppermute | solution.py:56
  26.4 5.2 %collective-permute-start.5 = (bf16[16,4608]{1,0:T(8,128)(2,1)S(1)}, bf16[16,4608]{1,0:T(8,128)(2,1)S(1)}, u32[]{:S(2)}, u32[]{:S(2)}) collective-permute-start(bf16[16,4608]{1,0:T(8,128)(2,1)S(1)} %collective-permute-done.4), channel_id=1, source_target_pairs={{0,2},{1,5},{2,0},{3,7},{4,6},{5,1},{6,4},{7,3},{8,10},{9,13},{10,... | collective-permute-start | bytes 442376 | tf_op jit(solution)/shard_map/ppermute | solution.py:56
  28.3 12.1 %collective-permute-start.17 = (bf16[32,4992]{1,0:T(8,128)(2,1)S(1)}, bf16[32,4992]{1,0:T(8,128)(2,1)S(1)}, u32[]{:S(2)}, u32[]{:S(2)}) collective-permute-start(bf16[32,4992]{1,0:T(8,128)(2,1)S(1)} %pad_maximum_fusion.refs_0_.refs_4_), channel_id=1, source_target_pairs={{0,1},{1,0},{2,3},{3,2},{4,5},{5,4},{6,7},{7,6},{8,9},{9,8},{10,11... | collective-permute-start | bytes 958472 | tf_op jit(solution)/shard_map/ppermute | solution.py:60
  28.4 9.5 %collective-permute-start.13 = (bf16[32,4992]{1,0:T(8,128)(2,1)S(1)}, bf16[32,4992]{1,0:T(8,128)(2,1)S(1)}, u32[]{:S(2)}, u32[]{:S(2)}) collective-permute-start(bf16[32,4992]{1,0:T(8,128)(2,1)S(1)} %pad_maximum_fusion.refs_0_.refs_4_), channel_id=1, source_target_pairs={{0,2},{1,5},{2,0},{3,7},{4,6},{5,1},{6,4},{7,3},{8,10},{9,13},{10,... | collective-permute-start | bytes 958472 | tf_op jit(solution)/shard_map/ppermute | solution.py:56
  30.0 11.8 %collective-permute-start.16 = (bf16[32,4992]{1,0:T(8,128)(2,1)S(1)}, bf16[32,4992]{1,0:T(8,128)(2,1)}, u32[]{:S(2)}, u32[]{:S(2)}) collective-permute-start(bf16[32,4992]{1,0:T(8,128)(2,1)S(1)} %pad_maximum_fusion.refs_0_.refs_4_), channel_id=1, source_target_pairs={{0,5},{1,2},{2,7},{3,0},{4,1},{5,6},{6,3},{7,4},{8,13},{9,10},{10,... | collective-permute-start | bytes 958472 | tf_op jit(solution)/shard_map/ppermute | solution.py:56
  31.7 12.0 %collective-permute-start.6 = (bf16[32,4608]{1,0:T(8,128)(2,1)S(1)}, bf16[32,4608]{1,0:T(8,128)(2,1)}, u32[]{:S(2)}, u32[]{:S(2)}) collective-permute-start(bf16[32,4608]{1,0:T(8,128)(2,1)S(1)} %constant_dynamic-update-slice_fusion.refs_0_), channel_id=1, source_target_pairs={{0,4},{1,9},{2,6},{3,11},{4,0},{5,13},{6,2},{7,15},{8,12},{9,1},{1... | collective-permute-start | bytes 884744 | tf_op jit(solution)/shard_map/ppermute | solution.py:56
  37.8 6.7 %collective-permute-start.14 = (bf16[32,4992]{1,0:T(8,128)(2,1)S(1)}, bf16[32,4992]{1,0:T(8,128)(2,1)S(1)}, u32[]{:S(2)}, u32[]{:S(2)}) collective-permute-start(bf16[32,4992]{1,0:T(8,128)(2,1)S(1)} %collective-permute-done.13.refs_0_.refs_5_), channel_id=1, source_target_pairs={{0,5},{1,2},{2,7},{3,0},{4,1},{5,6},{6,3},{7,4},{8,13},{9,10},{10,... | collective-permute-start | bytes 958472 | tf_op jit(solution)/shard_map/ppermute | solution.py:56
  39.0 4.7 %collective-permute-start.20 = (bf16[32,4608]{1,0:T(8,128)(2,1)S(1)}, bf16[32,4608]{1,0:T(8,128)(2,1)S(1)}, u32[]{:S(2)}, u32[]{:S(2)}) collective-permute-start(bf16[32,4608]{1,0:T(8,128)(2,1)S(1)} %constant_dynamic-update-slice_fusion.refs_0_), channel_id=1, source_target_pairs={{0,1},{1,0},{2,3},{3,2},{4,5},{5,4},{6,7},{7,6},{8,9},{9,8},{10,11... | collective-permute-start | bytes 884744 | tf_op jit(solution)/shard_map/ppermute | solution.py:60
  41.2 7.8 %collective-permute-start.18 = (bf16[32,4992]{1,0:T(8,128)(2,1)S(1)}, bf16[32,4992]{1,0:T(8,128)(2,1)S(1)}, u32[]{:S(2)}, u32[]{:S(2)}) collective-permute-start(bf16[32,4992]{1,0:T(8,128)(2,1)S(1)} %collective-permute-done.13.refs_0_.refs_5_), channel_id=1, source_target_pairs={{0,1},{1,0},{2,3},{3,2},{4,5},{5,4},{6,7},{7,6},{8,9},{9,8},{10,11... | collective-permute-start | bytes 958472 | tf_op jit(solution)/shard_map/ppermute | solution.py:60
  41.9 6.3 %collective-permute-start.9 = (bf16[32,4608]{1,0:T(8,128)(2,1)S(1)}, bf16[32,4608]{1,0:T(8,128)(2,1)}, u32[]{:S(2)}, u32[]{:S(2)}) collective-permute-start(bf16[32,4608]{1,0:T(8,128)(2,1)S(1)} %constant_dynamic-update-slice_fusion.refs_0_), channel_id=1, source_target_pairs={{0,9},{1,2},{2,11},{3,0},{4,13},{5,6},{6,15},{7,4},{8,1},{9,10},{1... | collective-permute-start | bytes 884744 | tf_op jit(solution)/shard_map/ppermute | solution.py:56
  43.7 7.6 %collective-permute-start.7 = (bf16[32,4608]{1,0:T(8,128)(2,1)}, bf16[32,4608]{1,0:T(8,128)(2,1)}, u32[]{:S(2)}, u32[]{:S(2)}) collective-permute-start(bf16[32,4608]{1,0:T(8,128)(2,1)} %collective-permute-done.6.refs_0_), channel_id=1, source_target_pairs={{0,9},{1,2},{2,11},{3,0},{4,13},{5,6},{6,15},{7,4},{8,1},{9,10},{1... | collective-permute-start | bytes 884744 | tf_op jit(solution)/shard_map/ppermute | solution.py:56
  44.4 16.4 %collective-permute-start.19 = (bf16[32,4992]{1,0:T(8,128)(2,1)}, bf16[32,4992]{1,0:T(8,128)(2,1)}, u32[]{:S(2)}, u32[]{:S(2)}) collective-permute-start(bf16[32,4992]{1,0:T(8,128)(2,1)} %collective-permute-done.16.refs_0_.refs_6_), channel_id=1, source_target_pairs={{0,1},{1,0},{2,3},{3,2},{4,5},{5,4},{6,7},{7,6},{8,9},{9,8},{10,11... | collective-permute-start | bytes 958472 | tf_op jit(solution)/shard_map/ppermute | solution.py:60
  44.5 18.4 %collective-permute-start.15 = (bf16[32,4992]{1,0:T(8,128)(2,1)S(1)}, bf16[32,4992]{1,0:T(8,128)(2,1)}, u32[]{:S(2)}, u32[]{:S(2)}) collective-permute-start(bf16[32,4992]{1,0:T(8,128)(2,1)S(1)} %collective-permute-done.14.refs_0_.refs_7_), channel_id=1, source_target_pairs={{0,1},{1,0},{2,3},{3,2},{4,5},{5,4},{6,7},{7,6},{8,9},{9,8},{10,11... | collective-permute-start | bytes 958472 | tf_op jit(solution)/shard_map/ppermute | solution.py:60
  48.1 17.7 %collective-permute-start.11 = (bf16[32,4608]{1,0:T(8,128)(2,1)}, bf16[32,4608]{1,0:T(8,128)(2,1)}, u32[]{:S(2)}, u32[]{:S(2)}) collective-permute-start(bf16[32,4608]{1,0:T(8,128)(2,1)} %collective-permute-done.6.refs_0_), channel_id=1, source_target_pairs={{0,1},{1,0},{2,3},{3,2},{4,5},{5,4},{6,7},{7,6},{8,9},{9,8},{10,11... | collective-permute-start | bytes 884744 | tf_op jit(solution)/shard_map/ppermute | solution.py:60
  49.7 18.3 %collective-permute-start.10 = (bf16[32,4608]{1,0:T(8,128)(2,1)}, bf16[32,4608]{1,0:T(8,128)(2,1)}, u32[]{:S(2)}, u32[]{:S(2)}) collective-permute-start(bf16[32,4608]{1,0:T(8,128)(2,1)} %collective-permute-done.9.refs_0_), channel_id=1, source_target_pairs={{0,1},{1,0},{2,3},{3,2},{4,5},{5,4},{6,7},{7,6},{8,9},{9,8},{10,11... | collective-permute-start | bytes 884744 | tf_op jit(solution)/shard_map/ppermute | solution.py:60
  51.3 18.8 %collective-permute-start.8 = (bf16[32,4608]{1,0:T(8,128)(2,1)}, bf16[32,4608]{1,0:T(8,128)(2,1)}, u32[]{:S(2)}, u32[]{:S(2)}) collective-permute-start(bf16[32,4608]{1,0:T(8,128)(2,1)} %collective-permute-done.7.refs_0_), channel_id=1, source_target_pairs={{0,1},{1,0},{2,3},{3,2},{4,5},{5,4},{6,7},{7,6},{8,9},{9,8},{10,11... | collective-permute-start | bytes 884744 | tf_op jit(solution)/shard_map/ppermute | solution.py:60
  (13 other events, 22.3 us)
